TPU v7x, 256 devices: a whole 4x4x8 slice. The times are simulated.
256 devices in a mesh: sec: 2 (over y_hi), dev: 128 (over y_lo, x, z, core).
Axes of the slice: x: 4, y: 4 (y_hi: 2, y_lo: 2; y = y_hi * 2 + y_lo), z: 8, core: 2. Of those that a mesh axis runs over, the one named last changes fastest.
Arguments:
- hidden_in: bfloat16 [2, 1024, 6144], P(None, ('sec', 'dev')), may hold values from -30 to 30
- queries: bfloat16 [2, 1024, 6144], P(None, ('sec', 'dev')), may hold values from -5.2 to 5.2
- new_entries: bfloat16 [2, 1024, 2048], P(None, ('sec', 'dev')), may hold values from -5.2 to 5.2
- request_cache_rows: bfloat16 [1024, 192, 2048], P(('sec', 'dev')), may hold values from -5.2 to 5.2
- lengths: int32 [1024], P(('sec', 'dev')), may hold values from 1 to 192, as said below
- expert_ids: int32 [2, 1024, 2], P(None, ('sec', 'dev')), may hold values from 0 to 7, all different within a row; in each aligned block of 4 rows (0 to 3, 4 to 7, ..., all dimensions but the last counted through in order) at most 2 rows name the same one
- route_weights: float32 [2, 1024, 2], P(None, ('sec', 'dev')), may hold values from 0.25 to 1
- gate_weight: bfloat16 [2, 32768, 6144], P('sec', 'dev'), may hold values from -0.078125 to 0.078125
- up_weight: bfloat16 [2, 32768, 6144], P('sec', 'dev'), may hold values from -0.078125 to 0.078125
- down_weight: bfloat16 [2, 32768, 6144], P('sec', 'dev'), may hold values from -0.0625 to 0.0625
Outputs:
- attended: bfloat16 [2, 1024, 6144], P(None, ('sec', 'dev'))
- expert_mix: bfloat16 [2, 1024, 6144], P(None, ('sec', 'dev'))
Inputs may be any that keep to these rules, and one draw needn't show every extreme that they name: `lengths`: some request has exactly 192 cached positions. `expert_ids`: the two experts of a token differ. Among one device's tokens of one step (aligned blocks of 4 rows), no expert is named more than 2 times, a bound that some block reaches.
All inputs are finite; a program needn't handle non-finite values.
Results may differ from a plain program's by a relative error of at most 0.008.
Values may be sent and summed in bfloat16 or wider, within the bound.
A program may use at most 128 MiB of HBM per device.

v0:
```python
import math

import jax
import jax.numpy as jnp
from jax import lax
from jax.sharding import PartitionSpec as P

QUERY_HEADS = 48
KEY_VALUE_HEADS = 8
HEAD_SIZE = 128
E = 8
LONGEST_LENGTH = 192
CAP = 2


def attend(decode_step_index, queries, new_entries, request_cache_rows, lengths):
    request_list = request_cache_rows.shape[0]
    key_row_width = KEY_VALUE_HEADS * HEAD_SIZE
    query_group_width = QUERY_HEADS // KEY_VALUE_HEADS
    scale_factor = 1.0 / math.sqrt(HEAD_SIZE)
    query_current = queries[decode_step_index].reshape(
        request_list, KEY_VALUE_HEADS, query_group_width, HEAD_SIZE
    )
    cached_key_rows = request_cache_rows[:, :, :key_row_width].reshape(
        request_list, LONGEST_LENGTH, KEY_VALUE_HEADS, HEAD_SIZE
    )
    cached_value_rows = request_cache_rows[:, :, key_row_width:].reshape(
        request_list, LONGEST_LENGTH, KEY_VALUE_HEADS, HEAD_SIZE
    )
    newest_keys = new_entries[: decode_step_index + 1, :, :key_row_width].reshape(
        decode_step_index + 1, request_list, KEY_VALUE_HEADS, HEAD_SIZE
    )
    newest_values = new_entries[: decode_step_index + 1, :, key_row_width:].reshape(
        decode_step_index + 1, request_list, KEY_VALUE_HEADS, HEAD_SIZE
    )
    past_scores = (
        jnp.einsum(
            "rgqd,rpgd->rgqp", query_current, cached_key_rows, preferred_element_type=jnp.float32
        )
        * scale_factor
    )
    visible = jnp.arange(LONGEST_LENGTH, dtype=jnp.int32)[None, :] < lengths[:, None]
    past_scores = jnp.where(visible[:, None, None, :], past_scores, -jnp.inf)
    fresh_scores = (
        jnp.einsum(
            "rgqd,srgd->rgqs", query_current, newest_keys, preferred_element_type=jnp.float32
        )
        * scale_factor
    )
    row_max = jnp.maximum(jnp.max(past_scores, axis=-1), jnp.max(fresh_scores, axis=-1))[..., None]
    past_exp = jnp.exp(past_scores - row_max)
    fresh_exp = jnp.exp(fresh_scores - row_max)
    exp_sum = jnp.sum(past_exp, axis=-1, keepdims=True) + jnp.sum(fresh_exp, axis=-1, keepdims=True)
    past_weight = (past_exp / exp_sum).astype(jnp.bfloat16)
    fresh_weight = (fresh_exp / exp_sum).astype(jnp.bfloat16)
    mixed_heads = jnp.einsum(
        "rgqp,rpgd->rgqd", past_weight, cached_value_rows, preferred_element_type=jnp.float32
    )
    mixed_heads = mixed_heads + jnp.einsum(
        "rgqs,srgd->rgqd", fresh_weight, newest_values, preferred_element_type=jnp.float32
    )
    return mixed_heads.reshape(request_list, QUERY_HEADS * HEAD_SIZE).astype(jnp.bfloat16)


def place_slots(choices_now):
    choices_flat = choices_now.reshape(-1)
    onehot = (choices_flat[:, None] == jnp.arange(E, dtype=jnp.int32)[None, :]).astype(jnp.int32)
    earlier = jnp.cumsum(onehot, axis=0) - onehot
    position = choices_flat * CAP + jnp.sum(earlier * onehot, axis=1)
    return position.reshape(-1, 2)


def slot_buffer(normed, position):
    targets = jnp.arange(E * CAP, dtype=jnp.int32)
    selector = (targets[:, None] == position.reshape(-1)[None, :]).astype(jnp.bfloat16)
    doubled = jnp.repeat(normed, 2, axis=0)
    filled = jnp.dot(selector, doubled, preferred_element_type=jnp.float32).astype(jnp.bfloat16)
    return filled.reshape(E, CAP, normed.shape[1])


def half_partial(rows, gate_rows, up_rows, down_rows):
    feature_count = rows.shape[-1]
    flat_rows = rows.reshape(-1, feature_count)
    contract = (((1,), (1,)), ((), ()))
    gate_part = lax.dot_general(flat_rows, gate_rows, contract, preferred_element_type=jnp.float32)
    up_part = lax.dot_general(flat_rows, up_rows, contract, preferred_element_type=jnp.float32)
    activated = (jax.nn.silu(gate_part) * up_part).astype(jnp.bfloat16)
    partial_value = jnp.dot(activated, down_rows, preferred_element_type=jnp.float32).astype(
        jnp.bfloat16
    )
    return lax.optimization_barrier(partial_value).astype(jnp.float32).reshape(rows.shape)


def route_experts(outgoing, weight_sets):
    gate_set, up_set, down_set = weight_sets
    both_halves = lax.all_gather(
        lax.all_to_all(outgoing, "dev", split_axis=0, concat_axis=0, tiled=True)[None],
        "sec",
        axis=0,
        tiled=True,
    )
    partial_value = half_partial(both_halves, gate_set[0], up_set[0], down_set[0])
    paired_sum = lax.psum_scatter(
        partial_value.astype(jnp.bfloat16), "sec", scatter_dimension=0, tiled=True
    ).astype(jnp.float32)
    paired_rows = paired_sum[0].astype(jnp.bfloat16)
    return lax.all_to_all(paired_rows, "dev", split_axis=0, concat_axis=0, tiled=True)


def body(
    hidden_in,
    queries,
    new_entries,
    request_cache_rows,
    lengths,
    expert_ids,
    route_weights,
    gate_weight,
    up_weight,
    down_weight,
):
    groups_dev = lax.axis_size("dev") // E
    weight_sets = (gate_weight, up_weight, down_weight)
    attended_list = []
    mix_list = []
    for decode_step_index in range(2):
        attended_now = attend(decode_step_index, queries, new_entries, request_cache_rows, lengths)
        residual_sum = hidden_in[decode_step_index].astype(jnp.float32) + attended_now.astype(
            jnp.float32
        )
        mean_square = jnp.mean(residual_sum * residual_sum, axis=-1, keepdims=True)
        normed = (residual_sum * lax.rsqrt(mean_square + 1e-05)).astype(jnp.bfloat16)
        prepare_position = place_slots(expert_ids[decode_step_index])
        outgoing = jnp.repeat(slot_buffer(normed, prepare_position), groups_dev, axis=0)
        attended_now, position, outgoing = (attended_now, prepare_position, outgoing)
        returned_rows = route_experts(outgoing, weight_sets)
        attended_list.append(attended_now)
        slot_count = returned_rows.shape[1]
        summed = jnp.sum(
            returned_rows.reshape(E, groups_dev, slot_count, returned_rows.shape[2]).astype(
                jnp.float32
            ),
            axis=1,
        )
        targets = jnp.arange(E * CAP, dtype=jnp.int32)
        combine = jnp.sum(
            (position[:, :, None] == targets[None, None, :]).astype(jnp.float32)
            * route_weights[decode_step_index][:, :, None],
            axis=1,
        )
        mixture = jnp.dot(
            combine,
            summed.reshape(E * CAP, -1),
            precision=lax.Precision.HIGHEST,
            preferred_element_type=jnp.float32,
        )
        mix_list.append(mixture.astype(jnp.bfloat16))
    return (jnp.stack(attended_list), jnp.stack(mix_list))


def solution(mesh):
    placed = (
        P(None, ("sec", "dev"), None),
        P(None, ("sec", "dev"), None),
        P(None, ("sec", "dev"), None),
        P(("sec", "dev"), None, None),
        P(("sec", "dev")),
        P(None, ("sec", "dev"), None),
        P(None, ("sec", "dev"), None),
        P("sec", "dev", None),
        P("sec", "dev", None),
        P("sec", "dev", None),
    )
    return jax.shard_map(
        body,
        mesh=mesh,
        in_specs=placed,
        out_specs=(P(None, ("sec", "dev"), None), P(None, ("sec", "dev"), None)),
        check_vma=False,
    )
```

profile of v0, /device:TPU:1, one launch (start us, length us, event | category | flops | bytes accessed | tf_op | source)
XLA Modules:
  0.0 644.2 jit_solution(6433894327325342001)
XLA Ops:
  7.2 0.9 fusion.79
  8.1 1.4 convert_bitcast_fusion
  9.5 0.9 fusion.78
  11.0 3.9 slice_bitcast_fusion
  15.3 0.9 copy-done.1
  16.1 1.0 fusion.81
  18.1 3.0 fusion.83
  22.0 1.2 fusion.60
  23.8 1.3 copy.160
  25.1 1.3 fusion.80
  26.7 0.7 select_reduce_fusion.1
  28.2 1.0 fusion.67
  29.2 2.6 fusion.54
  33.1 0.9 reshape.236
  34.3 0.7 multiply_convert_fusion.1
  35.5 3.6 broadcast_in_dim.60
  39.0 15.3 %all-to-all-start.2 = ((bf16[128,2,6144]{2,1,0:T(2,128)(2,1)}), bf16[128,2,6144]{2,1,0:T(2,128)(2,1)}, u32[]{:S(2)}, u32[]{:S(2)}) async-start(bf16[128,2,6144]{2,1,0:T(2,128)(2,1)} %bitcast.112), calls=%async_computation.3 | async-start | bytes 6291456 | tf_op jit(solution)/shard_map/all_to_all | solution.py:97
  55.0 72.1 %all-to-all-done.2 = bf16[128,2,6144]{2,1,0:T(2,128)(2,1)} async-done(((bf16[128,2,6144]{2,1,0:T(2,128)(2,1)}), bf16[128,2,6144]{2,1,0:T(2,128)(2,1)}, u32[]{:S(2)}, u32[]{:S(2)}) %all-to-all-start.2) | async-done | bytes 3145760 | tf_op jit(solution)/shard_map/all_to_all | solution.py:97
  127.5 1.9 broadcast_in_dim.31
  129.4 81.4 %all_to_all.20 = bf16[128,2,6144]{2,1,0:T(2,128)(2,1)} all-to-all(bf16[128,2,6144]{2,1,0:T(2,128)(2,1)S(1)} %bitcast.113), channel_id=1, replica_groups=mesh['sec'=2,'dev'=128] {'dev'}, dimensions={0} | all-to-all | bytes 6291456 | tf_op jit(solution)/shard_map/all_to_all | solution.py:97
  210.9 33.2 %all-gather.7.cloned.1.call-done = bf16[256,2,6144]{2,1,0:T(2,128)(2,1)} async-done(((bf16[128,2,6144]{2,1,0:T(2,128)(2,1)}), bf16[256,2,6144]{2,1,0:T(2,128)(2,1)}) %all-gather.7.cloned.1.call-update) | async-done | bytes 6291472 | tf_op jit(solution)/shard_map/all_gather | solution.py:96
  244.0 13.3 %reshape.229 = bf16[512,6144]{1,0:T(8,128)(2,1)} reshape(bf16[256,2,6144]{2,1,0:T(2,128)(2,1)} %all-gather.7.cloned.1.call-done) | data formatting | bytes 12582912 | tf_op jit(solution)/shard_map/reshape | solution.py:83
  257.3 6.8 %fusion.8 = f32[512,256]{1,0:T(8,128)S(1)} fusion(bf16[512,6144]{1,0:T(8,128)(2,1)} %reshape.229, bf16[1,256,6144]{2,1,0:T(8,128)(2,1)} %param.17), kind=kOutput, calls=%fused_computation.16 | convolution fusion | flops 1610612736 | bytes 9961472 | tf_op jit(solution)/shard_map/dot_general | solution.py:85
  264.6 1.2 copy-done.22
  265.7 1.8 fusion.30
  267.6 4.5 convolution_convert_fusion
  272.0 12.8 %convert_element_type.168 = bf16[2,128,2,6144]{3,2,1,0:T(2,128)(2,1)} reshape(bf16[512,6144]{1,0:T(8,128)(2,1)} %convolution_convert_fusion) | data formatting | bytes 12582912 | tf_op jit(solution)/shard_map/convert_element_type | solution.py:104
  284.9 8.0 %copy.106 = bf16[2,128,2,6144]{3,1,2,0:T(8,128)(2,1)} copy(bf16[2,128,2,6144]{3,2,1,0:T(2,128)(2,1)} %convert_element_type.168) | data formatting | bytes 12582912 | tf_op jit(solution)/shard_map/convert_element_type | solution.py:104
  293.2 37.6 %all-gather.5.cloned.1.call-done = bf16[256,2,6144]{2,1,0:T(2,128)(2,1)} async-done(((bf16[128,2,6144]{2,1,0:T(2,128)(2,1)}), bf16[256,2,6144]{2,1,0:T(2,128)(2,1)}) %all-gather.5.cloned.1.call-update) | async-done | bytes 6291472 | tf_op jit(solution)/shard_map/all_gather | solution.py:96
  330.7 13.3 %reshape.224 = bf16[512,6144]{1,0:T(8,128)(2,1)} reshape(bf16[256,2,6144]{2,1,0:T(2,128)(2,1)} %all-gather.5.cloned.1.call-done) | data formatting | bytes 12582912 | tf_op jit(solution)/shard_map/reshape | solution.py:83
  344.0 6.3 fusion.10
  350.4 0.8 copy-done.23
  351.2 1.8 fusion.33
  353.0 4.5 convolution_convert_fusion.1
  357.4 13.2 %convert_element_type.154 = bf16[2,128,2,6144]{3,2,1,0:T(2,128)(2,1)} reshape(bf16[512,6144]{1,0:T(8,128)(2,1)} %convolution_convert_fusion.1) | data formatting | bytes 12582912 | tf_op jit(solution)/shard_map/convert_element_type | solution.py:104
  370.7 8.1 %copy.100 = bf16[2,128,2,6144]{3,1,2,0:T(8,128)(2,1)} copy(bf16[2,128,2,6144]{3,2,1,0:T(2,128)(2,1)} %convert_element_type.154) | data formatting | bytes 12582912 | tf_op jit(solution)/shard_map/convert_element_type | solution.py:104
  378.8 37.7 %reduce-scatter.5.cloned.1.call-done = bf16[1,128,2,6144]{3,1,2,0:T(8,128)(2,1)} async-done(((bf16[2,128,2,6144]{3,1,2,0:T(8,128)(2,1)}), bf16[1,128,2,6144]{3,1,2,0:T(8,128)(2,1)}) %reduce-scatter.5.cloned.1.call-update) | async-done | bytes 3145744 | tf_op jit(solution)/shard_map/reduce_scatter | solution.py:103
  416.5 6.8 %copy.107 = bf16[128,2,6144]{2,1,0:T(2,128)(2,1)} copy(bf16[128,2,6144]{2,0,1:T(8,128)(2,1)} %bitcast.114) | data formatting | bytes 6291456 | tf_op jit(solution)/shard_map/convert_element_type | solution.py:106
  423.3 12.0 %all-to-all-start.3 = ((bf16[128,2,6144]{2,1,0:T(2,128)(2,1)}), bf16[128,2,6144]{2,1,0:T(2,128)(2,1)}, u32[]{:S(2)}, u32[]{:S(2)}) async-start(bf16[128,2,6144]{2,1,0:T(2,128)(2,1)} %copy.107), calls=%async_computation.5 | async-start | bytes 6291456 | tf_op jit(solution)/shard_map/all_to_all | solution.py:107
  435.3 100.5 %reduce-scatter.3.cloned.1.call-done = bf16[1,128,2,6144]{3,1,2,0:T(8,128)(2,1)} async-done(((bf16[2,128,2,6144]{3,1,2,0:T(8,128)(2,1)}), bf16[1,128,2,6144]{3,1,2,0:T(8,128)(2,1)}) %reduce-scatter.3.cloned.1.call-update) | async-done | bytes 3145744 | tf_op jit(solution)/shard_map/reduce_scatter | solution.py:103
  535.8 6.8 %copy.101 = bf16[128,2,6144]{2,1,0:T(2,128)(2,1)} copy(bf16[128,2,6144]{2,0,1:T(8,128)(2,1)} %bitcast.115) | data formatting | bytes 6291456 | tf_op jit(solution)/shard_map/convert_element_type | solution.py:106
  542.6 12.3 %all-to-all-start.1 = ((bf16[128,2,6144]{2,1,0:T(2,128)(2,1)}), bf16[128,2,6144]{2,1,0:T(2,128)(2,1)}, u32[]{:S(2)}, u32[]{:S(2)}) async-start(bf16[128,2,6144]{2,1,0:T(2,128)(2,1)} %copy.101), calls=%async_computation.2 | async-start | bytes 6291456 | tf_op jit(solution)/shard_map/all_to_all | solution.py:107
  556.2 5.4 convert_reduce_fusion
  561.6 1.3 reshape.230
  562.9 64.8 %all-to-all-done.1 = bf16[128,2,6144]{2,1,0:T(2,128)(2,1)} async-done(((bf16[128,2,6144]{2,1,0:T(2,128)(2,1)}), bf16[128,2,6144]{2,1,0:T(2,128)(2,1)}, u32[]{:S(2)}, u32[]{:S(2)}) %all-to-all-start.1) | async-done | bytes 3145760 | tf_op jit(solution)/shard_map/all_to_all | solution.py:107
  627.7 5.4 convert_reduce_fusion.1
  633.1 2.0 reshape.225
  635.4 1.3 fusion
  (105 shorter events, 10.4 us)
Async XLA Ops:
  7.2 260.4 %copy-start = (bf16[1,256,6144]{2,1,0:T(8,128)(2,1)S(1)}, bf16[1,256,6144]{2,1,0:T(8,128)(2,1)}, u32[]{:S(2)}) copy-start(bf16[1,256,6144]{2,1,0:T(8,128)(2,1)} %param.19) | copy-start | bytes 9437188
  11.0 3.9 copy-start.24
  15.0 1.2 copy-start.1
  15.1 3.0 copy-start.18
  15.2 2.8 copy-start.11
  26.6 0.9 copy-start.16
  26.7 5.1 copy-start.4
  26.7 5.1 copy-start.5
  26.7 5.1 copy-start.12
  26.7 5.1 copy-start.13
  26.7 5.1 copy-start.14
  28.2 5.9 copy-start.6
  29.2 5.9 copy-start.17
  29.2 5.9 copy-start.20
  32.4 0.6 copy-start.8
  39.0 15.4 %copy-start.19 = (s32[1,4,2]{1,2,0:T(2,128)S(1)}, s32[1,4,2]{1,2,0:T(2,128)}, u32[]{:S(2)}) copy-start(s32[1,4,2]{1,2,0:T(2,128)} %get-tuple-element.18) | copy-start | bytes 100
  39.0 15.7 %copy-start.10 = (bf16[4,6144]{1,0:T(4,128)(2,1)S(1)}, bf16[4,6144]{1,0:T(4,128)(2,1)}, u32[]{:S(2)}) copy-start(bf16[4,6144]{1,0:T(4,128)(2,1)} %get-tuple-element.6) | copy-start | bytes 147460
  39.0 88.1 %all-to-all-start.2 = ((bf16[128,2,6144]{2,1,0:T(2,128)(2,1)}), bf16[128,2,6144]{2,1,0:T(2,128)(2,1)}, u32[]{:S(2)}, u32[]{:S(2)}) async-start(bf16[128,2,6144]{2,1,0:T(2,128)(2,1)} %bitcast.112), calls=%async_computation.3 | async-start | bytes 6291456 | tf_op jit(solution)/shard_map/all_to_all | solution.py:97
  54.4 189.7 %all-gather.7.cloned.1.call-start = ((), (), s32[]{:S(2)}) async-start(), calls=%async_computation.9 | async-start | bytes 9437184 | tf_op jit(solution)/shard_map/all_gather | solution.py:96
  127.1 203.6 %all-gather.5.cloned.1.call-start = ((), (), s32[]{:S(2)}) async-start(), calls=%async_computation.8 | async-start | bytes 9437184 | tf_op jit(solution)/shard_map/all_gather | solution.py:96
  210.8 205.7 %reduce-scatter.5.cloned.1.call-start = ((), (), s32[]{:S(2)}) async-start(), calls=%async_computation.7 | async-start | bytes 9437184 | tf_op jit(solution)/shard_map/reduce_scatter | solution.py:103
  257.3 7.2 %copy-start.2 = (bf16[512,6144]{1,0:T(8,128)(2,1)S(1)}, bf16[512,6144]{1,0:T(8,128)(2,1)}, u32[]{:S(2)}) copy-start(bf16[512,6144]{1,0:T(8,128)(2,1)} %reshape.229) | copy-start | bytes 18874372
  257.3 8.4 %copy-start.22 = (bf16[1,256,6144]{2,1,0:T(8,128)(2,1)S(1)}, bf16[1,256,6144]{2,1,0:T(8,128)(2,1)}, u32[]{:S(2)}) copy-start(bf16[1,256,6144]{2,1,0:T(8,128)(2,1)} %param.18) | copy-start | bytes 9437188
  292.9 242.9 %reduce-scatter.3.cloned.1.call-start = ((), (), s32[]{:S(2)}) async-start(), calls=%async_computation.6 | async-start | bytes 9437184 | tf_op jit(solution)/shard_map/reduce_scatter | solution.py:103
  344.0 6.3 copy-start.3
  344.0 7.1 %copy-start.23 = (bf16[1,256,6144]{2,1,0:T(8,128)(2,1)S(1)}, bf16[1,256,6144]{2,1,0:T(8,128)(2,1)}, u32[]{:S(2)}) copy-start(bf16[1,256,6144]{2,1,0:T(8,128)(2,1)} %param.18) | copy-start | bytes 9437188
  423.3 119.3 %all-to-all-start.3 = ((bf16[128,2,6144]{2,1,0:T(2,128)(2,1)}), bf16[128,2,6144]{2,1,0:T(2,128)(2,1)}, u32[]{:S(2)}, u32[]{:S(2)}) async-start(bf16[128,2,6144]{2,1,0:T(2,128)(2,1)} %copy.107), calls=%async_computation.5 | async-start | bytes 6291456 | tf_op jit(solution)/shard_map/all_to_all | solution.py:107
  542.6 12.4 %copy-start.7 = (bf16[4,8,6,128]{3,2,1,0:T(8,128)(2,1)S(1)}, bf16[4,8,6,128]{3,2,1,0:T(8,128)(2,1)}, u32[]{:S(2)}) copy-start(bf16[4,8,6,128]{3,2,1,0:T(8,128)(2,1)} %fusion.54) | copy-start | bytes 147460
  542.6 12.4 %copy-start.9 = (bf16[4,8,6,128]{3,2,1,0:T(8,128)(2,1)S(1)}, bf16[4,8,6,128]{3,2,1,0:T(8,128)(2,1)}, u32[]{:S(2)}) copy-start(bf16[4,8,6,128]{3,2,1,0:T(8,128)(2,1)} %copy-done.8) | copy-start | bytes 147460
  542.6 12.8 %copy-start.21 = (f32[2,4,2]{1,2,0:T(2,128)S(1)}, f32[2,4,2]{1,2,0:T(2,128)}, u32[]{:S(2)}) copy-start(f32[2,4,2]{1,2,0:T(2,128)} %param.16) | copy-start | bytes 196
  542.6 12.8 %copy-start.15 = (s32[2,4,2]{1,2,0:T(2,128)S(1)}, s32[2,4,2]{1,2,0:T(2,128)}, u32[]{:S(2)}) copy-start(s32[2,4,2]{1,2,0:T(2,128)} %param.15) | copy-start | bytes 196
  542.6 85.1 %all-to-all-start.1 = ((bf16[128,2,6144]{2,1,0:T(2,128)(2,1)}), bf16[128,2,6144]{2,1,0:T(2,128)(2,1)}, u32[]{:S(2)}, u32[]{:S(2)}) async-start(bf16[128,2,6144]{2,1,0:T(2,128)(2,1)} %copy.101), calls=%async_computation.2 | async-start | bytes 6291456 | tf_op jit(solution)/shard_map/all_to_all | solution.py:107
Sparse Core Ops, SparseCore 0:
  127.3 116.7 all-gather.6
  245.8 84.8 all-gather.4
  333.3 83.1 reduce-scatter.4
  418.9 116.8 reduce-scatter.2
where the time goes:
time: 655 us; the launch traced here: 644 us
  waiting for transfers between devices  346 us (53%)
  local copies, waits for them, and re-layouts  107 us (16%)
  blocking collectives  81.4 us (12%)
  starting transfers between devices  40.1 us (6%)
  matrix products  36.2 us (6%)
  other arithmetic  19.2 us (3%)
  between operations  14.4 us (2%)
    reduce_scatter x2, waiting for transfers between devices, route_experts(): lax.psum_scatter(partial_value.astype(jnp.bfloat16), 'sec', scatter_dimen...  138 us
    all_to_all x1, blocking collectives, route_experts(): lax.all_to_all(outgoing, 'dev', split_axis=0, concat_axis=0, tiled=True)  81.4 us
    all_to_all x1, waiting for transfers between devices, route_experts(): lax.all_to_all(outgoing, 'dev', split_axis=0, concat_axis=0, tiled=True)  72.1 us
    all_gather x2, waiting for transfers between devices, route_experts(): lax.all_gather(lax.all_to_all(outgoing, 'dev', split_axis=0, concat_axis=...  70.7 us
    all_to_all x2, waiting for transfers between devices, route_experts(): lax.all_to_all(paired_rows, 'dev', split_axis=0, concat_axis=0, tiled=True)  64.8 us
    convert_element_type x4, local copies, waits for them, and re-layouts, route_experts(): partial_value.astype(jnp.bfloat16)  42.2 us
    reshape x2, local copies, waits for them, and re-layouts, half_partial(): flat_rows = rows.reshape(-1, feature_count)  26.6 us
    all_to_all x2, starting transfers between devices, route_experts(): lax.all_to_all(paired_rows, 'dev', split_axis=0, concat_axis=0, tiled=True)  24.4 us
  transfers between devices with their start and end apart: 7, of which 6 were waited for; matrix products, arithmetic and copies ran while one was open for 18% of the time, Pallas kernels for 0%

commit v1 on v0

v1 whole, which is shorter than its diff:
```python
import functools
import math

import jax
import jax.numpy as jnp
from jax import lax
from jax.experimental import pallas as pl
from jax.experimental.pallas import tpu as pltpu
from jax.sharding import PartitionSpec as P

QUERY_HEADS = 48
KEY_VALUE_HEADS = 8
HEAD_SIZE = 128
E = 8
LONGEST_LENGTH = 192
CAP = 2
STEPS = 2
GROUP = QUERY_HEADS // KEY_VALUE_HEADS
PADDED_GROUP = 8
FRESH_ROWS = 16
RING = 8
LANE = 2 * RING
SLOTS = STEPS * CAP
MESH = pl.DeviceIdType.MESH
CONTRACT_LAST = (((1,), (1,)), ((), ()))


def attend_kernel(lengths_ref, q_ref, fresh_ref, cache_ref, out_ref):
    rows = STEPS * PADDED_GROUP
    key_width = KEY_VALUE_HEADS * HEAD_SIZE
    scale = 1.0 / math.sqrt(HEAD_SIZE)
    length = lengths_ref[pl.program_id(0)]
    visible = lax.broadcasted_iota(jnp.int32, (rows, LONGEST_LENGTH), 1) < length
    row = lax.broadcasted_iota(jnp.int32, (rows, FRESH_ROWS), 0)
    column = lax.broadcasted_iota(jnp.int32, (rows, FRESH_ROWS), 1)
    fresh_visible = column <= row // PADDED_GROUP
    for head in range(KEY_VALUE_HEADS):
        keys = pl.ds(head * HEAD_SIZE, HEAD_SIZE)
        values = pl.ds(key_width + head * HEAD_SIZE, HEAD_SIZE)
        q = q_ref[0, head]
        past = lax.dot_general(
            q, cache_ref[0, :, keys], CONTRACT_LAST, preferred_element_type=jnp.float32
        )
        past = jnp.where(visible, past * scale, -jnp.inf)
        fresh = lax.dot_general(
            q, fresh_ref[0, :, keys], CONTRACT_LAST, preferred_element_type=jnp.float32
        )
        fresh = jnp.where(fresh_visible, fresh * scale, -jnp.inf)
        top = jnp.maximum(
            jnp.max(past, axis=1, keepdims=True), jnp.max(fresh, axis=1, keepdims=True)
        )
        past = jnp.exp(past - top)
        fresh = jnp.exp(fresh - top)
        total = jnp.sum(past, axis=1, keepdims=True) + jnp.sum(fresh, axis=1, keepdims=True)
        mixed = jnp.dot(
            (past / total).astype(jnp.bfloat16),
            cache_ref[0, :, values],
            preferred_element_type=jnp.float32,
        )
        mixed = mixed + jnp.dot(
            (fresh / total).astype(jnp.bfloat16),
            fresh_ref[0, :, values],
            preferred_element_type=jnp.float32,
        )
        out_ref[0, head] = mixed.astype(jnp.bfloat16)


def attend(queries, new_entries, request_cache_rows, lengths):
    requests = queries.shape[1]
    rows = STEPS * PADDED_GROUP
    width = request_cache_rows.shape[2]
    q = queries.reshape(STEPS, requests, KEY_VALUE_HEADS, GROUP, HEAD_SIZE)
    q = jnp.pad(q, ((0, 0), (0, 0), (0, 0), (0, PADDED_GROUP - GROUP), (0, 0)))
    q = q.transpose(1, 2, 0, 3, 4).reshape(requests, KEY_VALUE_HEADS, rows, HEAD_SIZE)
    fresh = jnp.pad(new_entries.transpose(1, 0, 2), ((0, 0), (0, FRESH_ROWS - STEPS), (0, 0)))
    heads_spec = pl.BlockSpec(
        (1, KEY_VALUE_HEADS, rows, HEAD_SIZE), lambda r, lengths_ref: (r, 0, 0, 0)
    )
    out = pl.pallas_call(
        attend_kernel,
        out_shape=jax.ShapeDtypeStruct(q.shape, jnp.bfloat16),
        grid_spec=pltpu.PrefetchScalarGridSpec(
            num_scalar_prefetch=1,
            grid=(requests,),
            in_specs=[
                heads_spec,
                pl.BlockSpec((1, FRESH_ROWS, width), lambda r, lengths_ref: (r, 0, 0)),
                pl.BlockSpec((1, LONGEST_LENGTH, width), lambda r, lengths_ref: (r, 0, 0)),
            ],
            out_specs=heads_spec,
        ),
        name="attend",
    )(lengths, q, fresh, request_cache_rows)
    out = out.reshape(requests, KEY_VALUE_HEADS, STEPS, PADDED_GROUP, HEAD_SIZE)[:, :, :, :GROUP]
    return out.transpose(2, 0, 1, 3, 4).reshape(STEPS, requests, QUERY_HEADS * HEAD_SIZE)


def plane_kernel(sections, columns, in_ref, out_ref, send_sem, recv_sem, own_sem):
    pieces = in_ref.shape[0]
    count = sections * columns
    device = lax.axis_index("dev")
    lane = device % LANE
    me = lax.axis_index("sec") * columns + device // LANE

    def place(peer):
        return (peer // columns, (peer % columns) * LANE + lane)

    barrier = pltpu.get_barrier_semaphore()
    for offset in range(1, count):
        pl.semaphore_signal(
            barrier, inc=1, device_id=place((me + offset) % count), device_id_type=MESH
        )
    own = pltpu.make_async_copy(in_ref.at[me % pieces], out_ref.at[me], own_sem)
    own.start()
    pl.semaphore_wait(barrier, count - 1)
    copies = []
    for offset in range(1, count):
        peer = (me + offset) % count
        copy = pltpu.make_async_remote_copy(
            src_ref=in_ref.at[peer % pieces],
            dst_ref=out_ref.at[me],
            send_sem=send_sem.at[offset - 1],
            recv_sem=recv_sem.at[offset - 1],
            device_id=place(peer),
            device_id_type=MESH,
        )
        copy.start()
        copies.append(copy)
    own.wait()
    for copy in copies:
        copy.wait()


def exchange_in_plane(pieces, sections, columns, collective_id, name):
    count = sections * columns
    return pl.pallas_call(
        functools.partial(plane_kernel, sections, columns),
        out_shape=jax.ShapeDtypeStruct((count,) + pieces.shape[1:], pieces.dtype),
        in_specs=[pl.BlockSpec(memory_space=pl.ANY)],
        out_specs=pl.BlockSpec(memory_space=pl.ANY),
        scratch_shapes=[
            pltpu.SemaphoreType.DMA((count - 1,)),
            pltpu.SemaphoreType.DMA((count - 1,)),
            pltpu.SemaphoreType.DMA,
        ],
        compiler_params=pltpu.CompilerParams(
            collective_id=collective_id, has_side_effects=True
        ),
        name=name,
    )(pieces)


def experts_kernel(
    block_ref,
    gate_ref,
    up_ref,
    down_ref,
    out_ref,
    gate,
    up,
    down,
    rows_0,
    rows_mid,
    rows_4,
    part_0,
    part_mid,
    part_4,
    other_0,
    other_mid,
    other_4,
    ring_3,
    ring_mid,
    gate_sum,
    up_sum,
    hidden,
    load_sem,
    gather_send,
    gather_recv,
    share_send,
    share_recv,
    pair_send,
    pair_recv,
    reduce_send,
    reduce_recv,
):
    size = block_ref.shape[0]
    half = size // 2
    features = block_ref.shape[1]
    wide = min(1024, features)
    narrow = min(512, features)
    section = lax.axis_index("sec")
    device = lax.axis_index("dev")
    column, z, core = device // LANE, (device % LANE) // 2, device % 2

    def at_z(where):
        return (section, column * LANE + (where % RING) * 2 + core)

    ahead, behind = at_z(z + 1), at_z(z + RING - 1)
    partner = (section, device + 1 - 2 * core)
    onward = (ahead, behind)
    back = (behind, ahead)

    def remote(source, target, send_sem, recv_sem, where):
        return pltpu.make_async_remote_copy(
            src_ref=source,
            dst_ref=target,
            send_sem=send_sem,
            recv_sem=recv_sem,
            device_id=where,
            device_id_type=MESH,
        )

    loads = [
        pltpu.make_async_copy(block_ref, rows_0.at[pl.ds(0, size)], load_sem.at[0]),
        pltpu.make_async_copy(gate_ref.at[0], gate, load_sem.at[1]),
        pltpu.make_async_copy(up_ref.at[0], up, load_sem.at[2]),
        pltpu.make_async_copy(down_ref.at[0], down, load_sem.at[3]),
    ]
    for load in loads:
        load.start()
    barrier = pltpu.get_barrier_semaphore()
    for where in (ahead, behind, partner):
        pl.semaphore_signal(barrier, inc=1, device_id=where, device_id_type=MESH)
    pl.semaphore_wait(barrier, 3)
    loads[0].wait()
    sends = []

    def start(copy):
        copy.start()
        sends.append(copy)
        return copy

    def rows_at(k, direction, h, of_partner=0):
        if k == 0:
            return rows_0.at[pl.ds(of_partner * size + h * half, half)]
        if k == 4:
            return rows_4.at[pl.ds(of_partner * size + h * half, half)]
        return rows_mid.at[
            k - 1, pl.ds(direction * 2 * size + of_partner * size + h * half, half)
        ]

    def gather(k, direction, h):
        return remote(
            rows_at(k - 1, direction, h),
            rows_at(k, direction, h),
            gather_send.at[k - 1, direction, h],
            gather_recv.at[k - 1, direction, h],
            onward[direction],
        )

    def share(k, direction, h):
        return remote(
            rows_at(k, direction, h),
            rows_at(k, direction, h, 1),
            share_send.at[k, direction, h],
            share_recv.at[k, direction, h],
            partner,
        )

    def chunks(k):
        if k == 0:
            return [(0, 0), (0, 1)]
        if k == 4:
            return [(0, 0), (1, 1)]
        return [(0, 0), (1, 0), (0, 1), (1, 1)]

    def multiply(rows, part):
        count = rows.shape[0]

        def features_step(i, carry):
            at = pl.ds(pl.multiple_of(i * wide, wide), wide)
            x = rows[:, at]
            gate_sum[pl.ds(0, count)] += lax.dot_general(
                x, gate[:, at], CONTRACT_LAST, preferred_element_type=jnp.float32
            )
            up_sum[pl.ds(0, count)] += lax.dot_general(
                x, up[:, at], CONTRACT_LAST, preferred_element_type=jnp.float32
            )
            return carry

        gate_sum[...] = jnp.zeros_like(gate_sum)
        up_sum[...] = jnp.zeros_like(up_sum)
        lax.fori_loop(0, features // wide, features_step, 0)
        value = gate_sum[pl.ds(0, count)]
        value = value / (1.0 + jnp.exp(-value)) * up_sum[pl.ds(0, count)]
        hidden[pl.ds(0, count)] = value.astype(jnp.bfloat16)

        def output_step(i, carry):
            at = pl.ds(pl.multiple_of(i * wide, wide), wide)
            part[:, at] = jnp.dot(
                hidden[pl.ds(0, count)], down[:, at], preferred_element_type=jnp.float32
            ).astype(jnp.bfloat16)
            return carry

        lax.fori_loop(0, features // wide, output_step, 0)

    def pair(k, direction):
        if k == 0:
            source, target = part_0.at[pl.ds(size, size)], other_0
        elif k == 4:
            source, target = part_4.at[pl.ds(size, size)], other_4
        else:
            source = part_mid.at[k - 1, pl.ds(direction * 2 * size + size, size)]
            target = other_mid.at[k - 1, pl.ds(direction * size, size)]
        return remote(
            source, target, pair_send.at[k, direction], pair_recv.at[k, direction], partner
        )

    def part_at(k, direction, h):
        if k == 4:
            return part_4.at[pl.ds(h * half, half)]
        return part_mid.at[k - 1, pl.ds(direction * 2 * size + h * half, half)]

    def other_at(k, direction, h):
        if k == 4:
            return other_4.at[pl.ds(h * half, half)]
        return other_mid.at[k - 1, pl.ds(direction * size + h * half, half)]

    def ring_at(k, direction, h):
        if k == 3:
            return ring_3.at[direction]
        return ring_mid.at[k, pl.ds(direction * size + h * half, half)]

    def reduce(k, direction, h):
        return remote(
            part_at(k, direction, h),
            ring_at(k - 1, direction, h),
            reduce_send.at[k - 1, direction, h],
            reduce_recv.at[k - 1, direction, h],
            back[direction],
        )

    def add(target, sources):
        def step(i, carry):
            at = pl.ds(pl.multiple_of(i * narrow, narrow), narrow)
            total = sources[0][:, at].astype(jnp.float32)
            for source in sources[1:]:
                total = total + source[:, at].astype(jnp.float32)
            target[:, at] = total.astype(jnp.bfloat16)
            return carry

        lax.fori_loop(0, features // narrow, step, 0)

    for h in range(2):
        for direction in range(2):
            start(gather(1, direction, h))
        start(share(0, 0, h))
    for load in loads[1:]:
        load.wait()
    for h in range(2):
        share(0, 0, h).wait_recv()
    multiply(rows_0, part_0)
    start(pair(0, 0))

    for k in range(1, 5):
        for direction, h in chunks(k):
            gather(k, direction, h).wait_recv()
            if k < 3 or (k == 3 and h == direction):
                start(gather(k + 1, direction, h))
            start(share(k, direction, h))
        for direction, h in chunks(k):
            share(k, direction, h).wait_recv()
        if k == 4:
            multiply(rows_4, part_4)
            start(pair(4, 0))
        else:
            multiply(rows_mid.at[k - 1], part_mid.at[k - 1])
            for direction in range(2):
                start(pair(k, direction))
        if k == 3:
            for direction in range(2):
                pair(3, direction).wait_recv()
                h = 1 - direction
                add(
                    part_at(3, direction, h),
                    [part_at(3, direction, h), other_at(3, direction, h)],
                )
                start(reduce(3, direction, h))

    pair(4, 0).wait_recv()
    for direction in range(2):
        h = direction
        add(part_at(4, direction, h), [part_at(4, direction, h), other_at(4, direction, h)])
        start(reduce(4, direction, h))
    for k in range(3, 0, -1):
        if k < 3:
            for direction in range(2):
                pair(k, direction).wait_recv()
        for other_half in range(2):
            for direction in range(2):
                h = direction if other_half else 1 - direction
                if k == 3 and not other_half:
                    continue
                reduce(k + 1, direction, h).wait_recv()
                add(
                    part_at(k, direction, h),
                    [
                        part_at(k, direction, h),
                        other_at(k, direction, h),
                        ring_at(k, direction, h),
                    ],
                )
                start(reduce(k, direction, h))
    pair(0, 0).wait_recv()
    for h in range(2):
        for direction in range(2):
            reduce(1, direction, h).wait_recv()
    add(
        out_ref,
        [
            part_0.at[pl.ds(0, size)],
            other_0,
            ring_mid.at[0, pl.ds(0, size)],
            ring_mid.at[0, pl.ds(size, size)],
        ],
    )
    for copy in sends:
        copy.wait_send()


def run_experts(block, gate_weight, up_weight, down_weight):
    size, features = block.shape
    units = gate_weight.shape[1]
    half = size // 2
    bf16 = jnp.bfloat16
    anywhere = pl.BlockSpec(memory_space=pl.ANY)
    return pl.pallas_call(
        experts_kernel,
        out_shape=jax.ShapeDtypeStruct((size, features), bf16),
        in_specs=[anywhere] * 4,
        out_specs=pl.BlockSpec(memory_space=pltpu.VMEM),
        scratch_shapes=[
            pltpu.VMEM((units, features), bf16),
            pltpu.VMEM((units, features), bf16),
            pltpu.VMEM((units, features), bf16),
            pltpu.VMEM((2 * size, features), bf16),
            pltpu.VMEM((3, 4 * size, features), bf16),
            pltpu.VMEM((2 * size, features), bf16),
            pltpu.VMEM((2 * size, features), bf16),
            pltpu.VMEM((3, 4 * size, features), bf16),
            pltpu.VMEM((2 * size, features), bf16),
            pltpu.VMEM((size, features), bf16),
            pltpu.VMEM((3, 2 * size, features), bf16),
            pltpu.VMEM((size, features), bf16),
            pltpu.VMEM((2, half, features), bf16),
            pltpu.VMEM((3, 2 * size, features), bf16),
            pltpu.VMEM((4 * size, units), jnp.float32),
            pltpu.VMEM((4 * size, units), jnp.float32),
            pltpu.VMEM((4 * size, units), bf16),
            pltpu.SemaphoreType.DMA((4,)),
            pltpu.SemaphoreType.DMA((4, 2, 2)),
            pltpu.SemaphoreType.DMA((4, 2, 2)),
            pltpu.SemaphoreType.DMA((5, 2, 2)),
            pltpu.SemaphoreType.DMA((5, 2, 2)),
            pltpu.SemaphoreType.DMA((5, 2)),
            pltpu.SemaphoreType.DMA((5, 2)),
            pltpu.SemaphoreType.DMA((4, 2, 2)),
            pltpu.SemaphoreType.DMA((4, 2, 2)),
        ],
        compiler_params=pltpu.CompilerParams(
            collective_id=1, has_side_effects=True, vmem_limit_bytes=60 * 1024 * 1024
        ),
        name="experts",
    )(block, gate_weight, up_weight, down_weight)


def body(
    sections,
    columns,
    hidden_in,
    queries,
    new_entries,
    request_cache_rows,
    lengths,
    expert_ids,
    route_weights,
    gate_weight,
    up_weight,
    down_weight,
):
    requests, features = hidden_in.shape[1:]
    attended = attend(queries, new_entries, request_cache_rows, lengths)
    residual_sum = hidden_in.astype(jnp.float32) + attended.astype(jnp.float32)
    mean_square = jnp.mean(residual_sum * residual_sum, axis=-1, keepdims=True)
    normed = (residual_sum * lax.rsqrt(mean_square + 1e-05)).astype(jnp.bfloat16)

    choices = expert_ids.reshape(STEPS, 2 * requests)
    same = choices[:, :, None] == choices[:, None, :]
    earlier = jnp.tril(jnp.ones((2 * requests, 2 * requests), jnp.bool_), -1)
    rank = jnp.sum((same & earlier[None]).astype(jnp.int32), axis=2)
    slot = choices * SLOTS + jnp.arange(STEPS, dtype=jnp.int32)[:, None] * CAP + rank
    slot = slot.reshape(STEPS * requests, 2)
    targets = jnp.arange(E * SLOTS, dtype=jnp.int32)
    chosen = slot[:, :, None] == targets[None, None, :]
    selector = jnp.any(chosen, axis=1).astype(jnp.bfloat16)
    combine = jnp.sum(
        chosen.astype(jnp.float32) * route_weights.reshape(STEPS * requests, 2)[:, :, None], axis=1
    )
    outgoing = lax.dot_general(
        selector,
        normed.reshape(STEPS * requests, features),
        (((0,), (0,)), ((), ())),
        preferred_element_type=jnp.float32,
    ).astype(jnp.bfloat16)

    arrived = exchange_in_plane(
        outgoing.reshape(E, SLOTS, features), sections, columns, 0, "dispatch"
    )
    block = arrived.reshape(sections * columns * SLOTS, features)
    reduced = run_experts(block, gate_weight, up_weight, down_weight)
    returned = exchange_in_plane(
        reduced.reshape(sections * columns, SLOTS, features), sections, columns, 2, "collect"
    )
    summed = jnp.sum(
        returned.reshape(sections, columns * SLOTS, features).astype(jnp.float32), axis=0
    )
    mixture = jnp.dot(
        combine,
        summed,
        precision=lax.Precision.HIGHEST,
        preferred_element_type=jnp.float32,
    )
    return attended, mixture.astype(jnp.bfloat16).reshape(STEPS, requests, features)


def solution(mesh):
    sections, columns = mesh.shape["sec"], mesh.shape["dev"] // LANE
    placed = (
        P(None, ("sec", "dev"), None),
        P(None, ("sec", "dev"), None),
        P(None, ("sec", "dev"), None),
        P(("sec", "dev"), None, None),
        P(("sec", "dev")),
        P(None, ("sec", "dev"), None),
        P(None, ("sec", "dev"), None),
        P("sec", "dev", None),
        P("sec", "dev", None),
        P("sec", "dev", None),
    )
    return jax.shard_map(
        functools.partial(body, sections, columns),
        mesh=mesh,
        in_specs=placed,
        out_specs=(P(None, ("sec", "dev"), None), P(None, ("sec", "dev"), None)),
        check_vma=False,
    )
```

time: 655 us -> 196 us (0.30); the launches traced: 644 us -> 196 us
  waiting for transfers between devices: 346 us -> 0 us
  Pallas kernels: 0 us -> 180 us
  local copies, waits for them, and re-layouts: 107 us -> 12.8 us
  blocking collectives: 81.4 us -> 0 us
  starting transfers between devices: 40.1 us -> 0 us
  matrix products: 36.2 us -> 0.8 us
  other arithmetic: 19.2 us -> 0.91 us
  between operations: 14.4 us -> 0.79 us
    pallas_call x0 -> x4, Pallas kernels: none -> 180 us  [the longest x1 133 us: run_experts(): pl.pallas_call(experts_kernel, out_shape=jax.ShapeDtypeStruct((size, feat...]
    reduce_scatter x2 -> x0, waiting for transfers between devices: 138 us -> none  [route_experts(): lax.psum_scatter(partial_value.astype(jnp.bfloat16), 'sec', scatter_dimen...]
    all_to_all x3 -> x0, waiting for transfers between devices: 137 us -> none  [the longest x1 72.1 us: route_experts(): lax.all_to_all(outgoing, 'dev', split_axis=0, concat_axis=0, tiled=True)]
    all_to_all x1 -> x0, blocking collectives: 81.4 us -> none  [route_experts(): lax.all_to_all(outgoing, 'dev', split_axis=0, concat_axis=0, tiled=True)]
    all_gather x2 -> x0, waiting for transfers between devices: 70.7 us -> none  [route_experts(): lax.all_gather(lax.all_to_all(outgoing, 'dev', split_axis=0, concat_axis=...]
    convert_element_type x10 -> x1, local copies, waits for them, and re-layouts: 56.7 us -> 1.5 us  [body(): returned.reshape(sections, columns * SLOTS, features).astype(jnp.float32)]
    all_to_all x3 -> x0, starting transfers between devices: 39.7 us -> none  [the longest x2 24.4 us: route_experts(): lax.all_to_all(paired_rows, 'dev', split_axis=0, concat_axis=0, tiled=True)]
    dot_general x17 -> x2, matrix products: 36.2 us -> 0.8 us  [the longest x1 0.49 us: body(): jnp.dot(combine, summed, precision=lax.Precision.HIGHEST, preferred_eleme...]
  transfers between devices with their start and end apart: 7 -> 0, of which waited for: 6 -> 0; matrix products, arithmetic and copies ran while one was open for 18% -> 0% of each run, Pallas kernels for 0% -> 0%
where the time goes in v1:
time: 196 us
  Pallas kernels  180 us (92%)
  local copies, waits for them, and re-layouts  12.8 us (7%)
    pallas_call x1, Pallas kernels, run_experts(): pl.pallas_call(experts_kernel, out_shape=jax.ShapeDtypeStruct((size, feat...  133 us
    pallas_call x2, Pallas kernels, exchange_in_plane(): pl.pallas_call(functools.partial(plane_kernel, sections, columns), out_sh...  32.2 us
    pallas_call x1, Pallas kernels, attend(): pl.pallas_call(attend_kernel, out_shape=jax.ShapeDtypeStruct(q.shape, jnp...  14.8 us

profile of v1, /device:TPU:1, one launch (start us, length us, event | category | flops | bytes accessed | tf_op | source)
XLA Modules:
  0.0 195.6 jit_solution(497808276813653813)
XLA Ops:
  0.6 0.0 copy-start.1
  0.6 0.0 copy-start.2
  0.6 0.8 copy.41
  1.5 0.7 pad.9.fresh_ref
  2.2 1.0 reshape.89
  3.2 0.7 copy_bitcast_fusion.1.q_ref
  3.9 14.8 %attend.1 = bf16[4,8,16,128]{3,2,1,0:T(8,128)(2,1)} custom-call(s32[4]{0:T(128)} %lengths_ref.1, bf16[4,8,16,128]{3,2,1,0:T(8,128)(2,1)} %copy_bitcast_fusion.1.q_ref, bf16[4,16,2048]{2,1,0:T(8,128)(2,1)} %pad.9.fresh_ref, bf16[4,192,2048]{2,1,0:T(8,128)(2,1)} %cache_ref.1), custom_call_target="tpu_custom_call" | custom-call | tf_op jit(solution)/shard_map/attend/pallas_call | solution.py:79
  18.7 0.9 copy_bitcast_fusion
  19.7 0.1 reshape.92
  19.7 0.0 copy-done.1
  19.7 0.0 copy-start
  19.8 0.2 multiply_reduce_fusion
  19.9 0.1 multiply_convert_fusion
  20.1 0.0 copy-done.2
  20.1 0.1 copy.34
  20.2 0.1 eq.28
  20.3 0.1 iota_compare_fusion.1
  20.4 0.2 convert_reduce_fusion
  20.6 0.1 reduce_sum.39
  20.7 0.1 copy.35
  20.7 0.1 mul.40
  20.8 0.1 add.47
  20.9 0.1 add.48
  21.0 0.1 fusion
  21.1 0.3 convolution_convert_fusion
  21.4 0.9 reshape.94.in_ref
  22.3 16.6 %dispatch.1 = bf16[16,4,6144]{2,1,0:T(4,128)(2,1)} custom-call(bf16[8,4,6144]{2,1,0:T(4,128)(2,1)} %reshape.94.in_ref), custom_call_target="tpu_custom_call" | custom-call | tf_op jit(solution)/shard_map/dispatch/pallas_call | solution.py:136
  38.9 2.3 %reshape.95.block_ref = bf16[64,6144]{1,0:T(8,128)(2,1)} reshape(bf16[16,4,6144]{2,1,0:T(4,128)(2,1)} %dispatch.1) | data formatting | bytes 1572864 | tf_op jit(solution)/shard_map/reshape | solution.py:509
  41.2 133.2 %experts.1 = bf16[64,6144]{1,0:T(8,128)(2,1)} custom-call(bf16[64,6144]{1,0:T(8,128)(2,1)} %reshape.95.block_ref, bf16[1,256,6144]{2,1,0:T(8,128)(2,1)} %gate_ref.1, bf16[1,256,6144]{2,1,0:T(8,128)(2,1)} %up_ref.1, bf16[1,256,6144]{2,1,0:T(8,128)(2,1)} %down_ref.1), custom_call_target="tpu_custom_call" | custom-call | tf_op jit(solution)/shard_map/experts/pallas_call | solution.py:427
  174.4 0.0 copy-done
  174.4 2.4 %reshape.96.in_ref = bf16[16,4,6144]{2,1,0:T(4,128)(2,1)} reshape(bf16[64,6144]{1,0:T(8,128)(2,1)} %experts.1) | data formatting | bytes 1572864 | tf_op jit(solution)/shard_map/reshape | solution.py:512
  176.8 0.0 copy-start.3
  176.8 15.7 %collect.1 = bf16[16,4,6144]{2,1,0:T(4,128)(2,1)} custom-call(bf16[16,4,6144]{2,1,0:T(4,128)(2,1)} %reshape.96.in_ref), custom_call_target="tpu_custom_call" | custom-call | tf_op jit(solution)/shard_map/collect/pallas_call | solution.py:136
  192.5 1.5 reshape.98
  194.0 0.2 reduce_sum.42
  194.2 0.0 copy-done.3
  194.2 0.1 mul.42
  194.3 0.1 select_reduce_fusion
  194.4 0.5 convolution_convert_fusion.1
  194.9 0.7 reshape.97
  (8 shorter events, 0.1 us)
Async XLA Ops:
  0.6 19.1 %copy-start.1 = (bf16[2,4,6144]{2,1,0:T(4,128)(2,1)S(1)}, bf16[2,4,6144]{2,1,0:T(4,128)(2,1)}, u32[]{:S(2)}) copy-start(bf16[2,4,6144]{2,1,0:T(4,128)(2,1)} %param.10) | copy-start | bytes 294916
  0.6 19.4 %copy-start.2 = (s32[2,4,2]{1,2,0:T(2,128)S(1)}, s32[2,4,2]{1,2,0:T(2,128)}, u32[]{:S(2)}) copy-start(s32[2,4,2]{1,2,0:T(2,128)} %param.15) | copy-start | bytes 196
  19.7 154.7 %copy-start = (bf16[2,4,6144]{2,1,0:T(4,128)(2,1)}, bf16[2,4,6144]{2,1,0:T(4,128)(2,1)S(1)}, u32[]{:S(2)}) copy-start(bf16[2,4,6144]{2,1,0:T(4,128)(2,1)S(1)} %reshape.92) | copy-start | bytes 294916
  176.8 17.4 %copy-start.3 = (f32[2,4,2]{1,2,0:T(2,128)S(1)}, f32[2,4,2]{1,2,0:T(2,128)}, u32[]{:S(2)}) copy-start(f32[2,4,2]{1,2,0:T(2,128)} %param.16) | copy-start | bytes 196

commit v2 on v1

v2 whole, which is shorter than its diff:
```python
import functools
import math

import jax
import jax.numpy as jnp
from jax import lax
from jax.experimental import pallas as pl
from jax.experimental.pallas import tpu as pltpu
from jax.sharding import PartitionSpec as P

QUERY_HEADS = 48
KEY_VALUE_HEADS = 8
HEAD_SIZE = 128
E = 8
LONGEST_LENGTH = 192
CAP = 2
STEPS = 2
GROUP = QUERY_HEADS // KEY_VALUE_HEADS
PADDED_GROUP = 8
RING = 8
LANE = 2 * RING
MESH = pl.DeviceIdType.MESH
CONTRACT_LAST = (((1,), (1,)), ((), ()))


def attend_kernel(lengths_ref, q_ref, fresh_ref, cache_ref, out_ref, cache, sem):
    requests = cache.shape[0]
    rows = STEPS * PADDED_GROUP
    key_width = KEY_VALUE_HEADS * HEAD_SIZE
    scale = 1.0 / math.sqrt(HEAD_SIZE)
    loads = [
        pltpu.make_async_copy(cache_ref.at[r], cache.at[r], sem.at[r]) for r in range(requests)
    ]
    for load in loads:
        load.start()
    every = KEY_VALUE_HEADS * rows
    place = lax.broadcasted_iota(jnp.int32, (every, LONGEST_LENGTH), 1)
    second = (lax.broadcasted_iota(jnp.int32, (every, 1), 0) // PADDED_GROUP) % STEPS == 1
    for r in range(requests):
        fresh_keys, fresh_values = [], []
        for t in range(STEPS):
            entry = fresh_ref[t, pl.ds(r, 1), :].astype(jnp.float32)
            fresh_keys.append(entry[:, :key_width])
            fresh_values.append(entry[:, key_width:])
        loads[r].wait()
        past, fresh = [], [[] for t in range(STEPS)]
        for head in range(KEY_VALUE_HEADS):
            lanes = slice(head * HEAD_SIZE, (head + 1) * HEAD_SIZE)
            q = q_ref[r, head]
            past.append(
                lax.dot_general(
                    q, cache[r, :, lanes], CONTRACT_LAST, preferred_element_type=jnp.float32
                )
            )
            wide = q.astype(jnp.float32)
            for t in range(STEPS):
                fresh[t].append(jnp.sum(wide * fresh_keys[t][:, lanes], axis=1, keepdims=True))
        past = jnp.concatenate(past, axis=0) * scale
        past = jnp.where(place < lengths_ref[r], past, -jnp.inf)
        fresh = [jnp.concatenate(part, axis=0) * scale for part in fresh]
        fresh[1] = jnp.where(second, fresh[1], -jnp.inf)
        top = jnp.maximum(jnp.max(past, axis=1, keepdims=True), jnp.maximum(fresh[0], fresh[1]))
        past = jnp.exp(past - top)
        fresh = [jnp.exp(part - top) for part in fresh]
        total = jnp.sum(past, axis=1, keepdims=True) + (fresh[0] + fresh[1])
        past = (past / total).astype(jnp.bfloat16)
        fresh = [(part / total).astype(jnp.bfloat16).astype(jnp.float32) for part in fresh]
        for head in range(KEY_VALUE_HEADS):
            lanes = slice(head * HEAD_SIZE, (head + 1) * HEAD_SIZE)
            values = slice(key_width + head * HEAD_SIZE, key_width + (head + 1) * HEAD_SIZE)
            here = slice(head * rows, (head + 1) * rows)
            mixed = jnp.dot(past[here], cache[r, :, values], preferred_element_type=jnp.float32)
            for t in range(STEPS):
                mixed = mixed + fresh[t][here] * fresh_values[t][:, lanes]
            out_ref[r, head] = mixed.astype(jnp.bfloat16)


def attend(queries, new_entries, request_cache_rows, lengths):
    requests = queries.shape[1]
    rows = STEPS * PADDED_GROUP
    q = queries.reshape(STEPS, requests, KEY_VALUE_HEADS, GROUP, HEAD_SIZE)
    q = jnp.pad(q, ((0, 0), (0, 0), (0, 0), (0, PADDED_GROUP - GROUP), (0, 0)))
    q = q.transpose(1, 2, 0, 3, 4).reshape(requests, KEY_VALUE_HEADS, rows, HEAD_SIZE)
    in_vmem = pl.BlockSpec(memory_space=pltpu.VMEM)
    out = pl.pallas_call(
        attend_kernel,
        out_shape=jax.ShapeDtypeStruct(q.shape, jnp.bfloat16),
        in_specs=[
            pl.BlockSpec(memory_space=pltpu.SMEM),
            in_vmem,
            in_vmem,
            pl.BlockSpec(memory_space=pl.ANY),
        ],
        out_specs=in_vmem,
        scratch_shapes=[
            pltpu.VMEM(request_cache_rows.shape, jnp.bfloat16),
            pltpu.SemaphoreType.DMA((requests,)),
        ],
        name="attend",
    )(lengths, q, new_entries, request_cache_rows)
    out = out.reshape(requests, KEY_VALUE_HEADS, STEPS, PADDED_GROUP, HEAD_SIZE)[:, :, :, :GROUP]
    return out.transpose(2, 0, 1, 3, 4).reshape(STEPS, requests, QUERY_HEADS * HEAD_SIZE)


def exchange_in_plane(
    sections, columns, both_out, own_out, both_in, own_in, send_sem, recv_sem, local_sem
):
    pieces = both_out.shape[0]
    count = sections * columns
    device = lax.axis_index("dev")
    lane = device % LANE
    section = lax.axis_index("sec")
    column = device // LANE
    me = section * columns + column
    copies = []

    def place(peer):
        return (peer // columns, (peer % columns) * LANE + lane)

    def greet():
        barrier = pltpu.get_barrier_semaphore()
        for offset in range(1, count):
            pl.semaphore_signal(
                barrier, inc=1, device_id=place((me + offset) % count), device_id_type=MESH
            )
        return lambda: pl.semaphore_wait(barrier, count - 1)

    def send(source, target, where):
        copies.append(
            pltpu.make_async_remote_copy(
                src_ref=source,
                dst_ref=target,
                send_sem=send_sem.at[len(copies)],
                recv_sem=recv_sem.at[len(copies)],
                device_id=where,
                device_id_type=MESH,
            )
        )
        copies[-1].start()

    def run():
        local = [
            pltpu.make_async_copy(both_out.at[me % pieces], both_in.at[me], local_sem.at[0]),
            pltpu.make_async_copy(own_out.at[column], own_in.at[column], local_sem.at[1]),
        ]
        for copy in local:
            copy.start()
        for offset in range(1, columns):
            peer = (column + offset) % columns
            send(own_out.at[peer], own_in.at[column], (section, peer * LANE + lane))
        for offset in range(1, count):
            peer = (me + offset) % count
            send(both_out.at[peer % pieces], both_in.at[me], place(peer))
        for copy in local + copies:
            copy.wait()

    return greet, run


def exchange_scratch(sections, columns, sent, features):
    count = sections * columns
    copies = count + columns - 2
    return [
        pltpu.VMEM((sent, CAP, features), jnp.bfloat16),
        pltpu.VMEM((columns, CAP, features), jnp.bfloat16),
        pltpu.VMEM((count, CAP, features), jnp.bfloat16),
        pltpu.VMEM((columns, CAP, features), jnp.bfloat16),
        pltpu.SemaphoreType.DMA((copies,)),
        pltpu.SemaphoreType.DMA((copies,)),
        pltpu.SemaphoreType.DMA((2,)),
    ]


def dispatch_kernel(
    sections, columns, attended_ref, hidden_ref, selector_ref, both_ref, own_ref, *scratch
):
    both_out, own_out, both_in, own_in = scratch[:4]
    greet, run = exchange_in_plane(sections, columns, *scratch)
    entered = greet()
    residual_sum = jnp.concatenate(
        [
            hidden_ref[t].astype(jnp.float32) + attended_ref[t].astype(jnp.float32)
            for t in range(STEPS)
        ],
        axis=0,
    )
    mean_square = jnp.mean(residual_sum * residual_sum, axis=-1, keepdims=True)
    normed = (residual_sum * lax.rsqrt(mean_square + 1e-05)).astype(jnp.bfloat16)
    slots = jnp.dot(selector_ref[...], normed, preferred_element_type=jnp.float32)
    slots = slots.astype(jnp.bfloat16)
    for e in range(columns):
        both_out[e] = slots[CAP * e : CAP * (e + 1)]
        own_out[e] = slots[CAP * (columns + e) : CAP * (columns + e + 1)]
    entered()
    run()
    for j in range(both_in.shape[0]):
        both_ref[pl.ds(CAP * j, CAP)] = both_in[j]
    for j in range(columns):
        own_ref[pl.ds(CAP * j, CAP)] = own_in[j]


def dispatch(attended, hidden_in, selector, sections, columns):
    features = attended.shape[-1]
    in_vmem = pl.BlockSpec(memory_space=pltpu.VMEM)
    return pl.pallas_call(
        functools.partial(dispatch_kernel, sections, columns),
        out_shape=(
            jax.ShapeDtypeStruct((sections * columns * CAP, features), jnp.bfloat16),
            jax.ShapeDtypeStruct((columns * CAP, features), jnp.bfloat16),
        ),
        in_specs=[in_vmem] * 3,
        out_specs=(in_vmem, in_vmem),
        scratch_shapes=exchange_scratch(sections, columns, columns, features),
        compiler_params=pltpu.CompilerParams(collective_id=0, has_side_effects=True),
        name="dispatch",
    )(attended, hidden_in, selector)


def collect_kernel(sections, columns, both_ref, own_ref, combine_ref, out_ref, rows, *scratch):
    both_out, own_out, both_in, own_in = scratch[:4]
    greet, run = exchange_in_plane(sections, columns, *scratch)
    entered = greet()
    for j in range(both_out.shape[0]):
        both_out[j] = both_ref[pl.ds(CAP * j, CAP)]
    for j in range(columns):
        own_out[j] = own_ref[pl.ds(CAP * j, CAP)]
    entered()
    run()
    count = both_in.shape[0]
    for j in range(count):
        rows[pl.ds(CAP * j, CAP)] = both_in[j]
    for j in range(columns):
        rows[pl.ds(CAP * (count + j), CAP)] = own_in[j]
    weights = combine_ref[...]
    parts = []
    for _ in range(3):
        part = weights.astype(jnp.bfloat16)
        weights = weights - part.astype(jnp.float32)
        parts.append(part)
    mixture = jnp.dot(parts[2], rows[...], preferred_element_type=jnp.float32)
    for part in (parts[1], parts[0]):
        mixture = mixture + jnp.dot(part, rows[...], preferred_element_type=jnp.float32)
    requests = out_ref.shape[1]
    for t in range(STEPS):
        out_ref[t] = mixture[t * requests : (t + 1) * requests].astype(jnp.bfloat16)


def collect(both, own, combine, sections, columns):
    features = both.shape[-1]
    requests = combine.shape[0] // STEPS
    in_vmem = pl.BlockSpec(memory_space=pltpu.VMEM)
    count = sections * columns
    return pl.pallas_call(
        functools.partial(collect_kernel, sections, columns),
        out_shape=jax.ShapeDtypeStruct((STEPS, requests, features), jnp.bfloat16),
        in_specs=[in_vmem] * 3,
        out_specs=in_vmem,
        scratch_shapes=[pltpu.VMEM(((count + columns) * CAP, features), jnp.bfloat16)]
        + exchange_scratch(sections, columns, count, features),
        compiler_params=pltpu.CompilerParams(collective_id=2, has_side_effects=True),
        name="collect",
    )(both, own, combine)


FIRST, AGAIN, OWN, CROSSED = 0, 1, 2, 3


def experts_kernel(
    both_ref,
    own_ref,
    gate_ref,
    up_ref,
    down_ref,
    both_out,
    own_out,
    gate,
    up,
    down,
    rows_0,
    rows_mid,
    rows_4,
    part_0,
    part_mid,
    part_4,
    other_0,
    other_mid,
    other_4,
    ring,
    crossed,
    hidden,
    load_sem,
    gather_send,
    gather_recv,
    share_send,
    share_recv,
    cross_send,
    cross_recv,
    pair_send,
    pair_recv,
    return_send,
    return_recv,
    reduce_send,
    reduce_recv,
):
    chunk = own_ref.shape[0]
    size = 4 * chunk
    features = own_ref.shape[1]
    wide = min(1024, features)
    narrow = min(512, features)
    section = lax.axis_index("sec")
    device = lax.axis_index("dev")
    column, z, core = device // LANE, (device % LANE) // 2, device % 2

    def at_z(where):
        return (section, column * LANE + ((where + RING) % RING) * 2 + core)

    sign = 1 - 2 * core
    onward = (at_z(z + sign), at_z(z - sign))
    back = (onward[1], onward[0])
    partner = (section, device + 1 - 2 * core)
    opposite = (1 - section, device)

    def remote(source, target, send_sem, recv_sem, where):
        return pltpu.make_async_remote_copy(
            src_ref=source,
            dst_ref=target,
            send_sem=send_sem,
            recv_sem=recv_sem,
            device_id=where,
            device_id_type=MESH,
        )

    loads = [
        pltpu.make_async_copy(own_ref, rows_0.at[pl.ds(OWN * chunk, chunk)], load_sem.at[0]),
        pltpu.make_async_copy(both_ref, rows_0.at[pl.ds(0, 2 * chunk)], load_sem.at[1]),
        pltpu.make_async_copy(gate_ref.at[0], gate, load_sem.at[2]),
        pltpu.make_async_copy(up_ref.at[0], up, load_sem.at[3]),
        pltpu.make_async_copy(down_ref.at[0], down, load_sem.at[4]),
    ]
    for load in loads:
        load.start()
    barrier = pltpu.get_barrier_semaphore()
    for where in onward + (partner, opposite):
        pl.semaphore_signal(barrier, inc=1, device_id=where, device_id_type=MESH)
    pl.semaphore_wait(barrier, 4)
    loads[0].wait()
    loads[1].wait()
    sends = []

    def start(copy):
        copy.start()
        sends.append(copy)

    def block_at(buffers, k, direction, c, of_partner=0):
        at = of_partner * size + c * chunk
        if k == 0:
            return buffers[0].at[pl.ds(at, chunk)]
        if k == 4:
            return buffers[2].at[pl.ds(at, chunk)]
        return buffers[1].at[k - 1, pl.ds(direction * 2 * size + at, chunk)]

    rows_at = functools.partial(block_at, (rows_0, rows_mid, rows_4))
    part_at = functools.partial(block_at, (part_0, part_mid, part_4))

    def gather(k, direction, c):
        return remote(
            rows_at(k - 1, direction, c),
            rows_at(k, direction, c),
            gather_send.at[k - 1, direction, c],
            gather_recv.at[k - 1, direction, c],
            onward[direction],
        )

    def share(k, direction, c):
        return remote(
            rows_at(k, direction, c),
            rows_at(k, direction, c, 1),
            share_send.at[k, direction, c],
            share_recv.at[k, direction, c],
            partner,
        )

    def cross(k, direction):
        return remote(
            rows_at(k, direction, OWN),
            rows_at(k, direction, CROSSED),
            cross_send.at[k, direction],
            cross_recv.at[k, direction],
            opposite,
        )

    def ringed(k):
        if k == 0:
            return []
        if k == 4:
            return [(1, OWN), (0, FIRST), (0, AGAIN)]
        return [(d, c) for c in (OWN, FIRST, AGAIN) for d in (0, 1)]

    def directions(k):
        return (0, 1) if 0 < k < 4 else (0,)

    def home(k, direction):
        return direction if 0 < k < 4 else 0

    def multiply(rows, part):
        count = rows.shape[0]

        x = rows[...]
        value = lax.dot_general(x, gate[...], CONTRACT_LAST, preferred_element_type=jnp.float32)
        value = value / (1.0 + jnp.exp(-value))
        value = value * lax.dot_general(
            x, up[...], CONTRACT_LAST, preferred_element_type=jnp.float32
        )
        hidden[pl.ds(0, count)] = value.astype(jnp.bfloat16)

        def output_step(i, carry):
            at = pl.ds(pl.multiple_of(i * wide, wide), wide)
            part[:, at] = jnp.dot(
                hidden[pl.ds(0, count)], down[:, at], preferred_element_type=jnp.float32
            ).astype(jnp.bfloat16)
            return carry

        lax.fori_loop(0, features // wide, output_step, 0)

    def pair(k, direction):
        if k == 0:
            source, target = part_0.at[pl.ds(size, size)], other_0
        elif k == 4:
            source, target = part_4.at[pl.ds(size, size)], other_4
        else:
            source = part_mid.at[k - 1, pl.ds(direction * 2 * size + size, size)]
            target = other_mid.at[k - 1, pl.ds(direction * size, size)]
        return remote(
            source, target, pair_send.at[k, direction], pair_recv.at[k, direction], partner
        )

    def other_at(k, direction, c):
        if k == 0:
            return other_0.at[pl.ds(c * chunk, chunk)]
        if k == 4:
            return other_4.at[pl.ds(c * chunk, chunk)]
        return other_mid.at[k - 1, pl.ds(direction * size + c * chunk, chunk)]

    def cross_back(k, direction):
        return remote(
            part_at(k, direction, CROSSED),
            crossed.at[k, direction],
            return_send.at[k, direction],
            return_recv.at[k, direction],
            opposite,
        )

    def ring_at(k, direction, c):
        return ring.at[k, direction, pl.ds(c * chunk, chunk)]

    def reduce(k, direction, c):
        return remote(
            part_at(k, direction, c),
            ring_at(k - 1, direction, c),
            reduce_send.at[k - 1, direction, c],
            reduce_recv.at[k - 1, direction, c],
            back[direction],
        )

    def add(target, sources):
        def step(i, carry):
            at = pl.ds(pl.multiple_of(i * narrow, narrow), narrow)
            total = sources[0][:, at].astype(jnp.float32)
            for source in sources[1:]:
                total = total + source[:, at].astype(jnp.float32)
            target[:, at] = total.astype(jnp.bfloat16)
            return carry

        lax.fori_loop(0, features // narrow, step, 0)

    def send_crossed_sums(k):
        for direction in directions(k):
            pair(k, direction).wait_recv()
            target = part_at(k, direction, CROSSED)
            add(target, [target, other_at(k, direction, CROSSED)])
            start(cross_back(k, direction))

    def send_sums(k, direction, c, from_ring=True):
        sources = [part_at(k, direction, c), other_at(k, direction, c)]
        if c == OWN:
            cross_back(k, home(k, direction)).wait_recv()
            sources.append(crossed.at[k, home(k, direction)])
        if from_ring:
            reduce(k + 1, direction, c).wait_recv()
            sources.append(ring_at(k, direction, c))
        add(sources[0], sources)
        start(reduce(k, direction, c))

    def take_in(k, arrivals):
        for direction, c in arrivals:
            gather(k, direction, c).wait_recv()
            if k < 3 or (k == 3 and (direction, c) in ringed(4)):
                start(gather(k + 1, direction, c))
            if c == OWN:
                start(cross(k, home(k, direction)))
            start(share(k, home(k, direction), c))

    def work_on(k):
        for direction in directions(k):
            cross(k, direction).wait_recv()
            start(share(k, direction, CROSSED))
        for direction in directions(k):
            for c in range(4):
                share(k, direction, c).wait_recv()
        if k == 0:
            multiply(rows_0, part_0)
        elif k == 4:
            multiply(rows_4, part_4)
        else:
            multiply(rows_mid.at[k - 1], part_mid.at[k - 1])
        for direction in directions(k):
            start(pair(k, direction))

    for c in (OWN, FIRST, AGAIN):
        for direction in range(2):
            start(gather(1, direction, c))
        if c == OWN:
            start(cross(0, 0))
        start(share(0, 0, c))

    take_in(1, ringed(1)[:2])
    for load in loads[2:]:
        load.wait()
    work_on(0)
    take_in(1, ringed(1)[2:])
    take_in(2, ringed(2)[:2])
    work_on(1)
    take_in(2, ringed(2)[2:])
    take_in(3, ringed(3)[:2])
    work_on(2)
    take_in(3, ringed(3)[2:])
    take_in(4, ringed(4)[:1])
    work_on(3)
    send_crossed_sums(3)
    take_in(4, ringed(4)[1:])
    for direction, c in ((1, FIRST), (1, AGAIN), (0, OWN)):
        send_sums(3, direction, c, from_ring=False)
    work_on(4)

    send_crossed_sums(4)
    send_sums(4, 0, FIRST, from_ring=False)
    send_sums(4, 0, AGAIN, from_ring=False)
    send_sums(4, 1, OWN, from_ring=False)
    send_crossed_sums(2)
    for c, direction in ((FIRST, 0), (AGAIN, 0), (OWN, 1)):
        send_sums(3, direction, c)
    send_crossed_sums(1)
    for k in (2, 1):
        for i in range(3):
            send_sums(k, 0, (OWN, FIRST, AGAIN)[i])
            send_sums(k, 1, (FIRST, AGAIN, OWN)[i])
        if k == 2:
            send_crossed_sums(0)
    for direction in range(2):
        for c in (FIRST, AGAIN, OWN):
            reduce(1, direction, c).wait_recv()
    cross_back(0, 0).wait_recv()
    own_rows = pl.ds(OWN * chunk, chunk)
    add(
        own_out,
        [
            part_0.at[own_rows],
            other_0.at[own_rows],
            crossed.at[0, 0],
            ring.at[0, 0, own_rows],
            ring.at[0, 1, own_rows],
        ],
    )
    both_rows = pl.ds(0, 2 * chunk)
    add(
        both_out,
        [
            part_0.at[both_rows],
            other_0.at[both_rows],
            ring.at[0, 0, both_rows],
            ring.at[0, 1, both_rows],
        ],
    )
    for copy in sends:
        copy.wait_send()


def run_experts(both, own, gate_weight, up_weight, down_weight):
    chunk, features = own.shape
    size = 4 * chunk
    units = gate_weight.shape[1]
    bf16 = jnp.bfloat16
    anywhere = pl.BlockSpec(memory_space=pl.ANY)
    in_vmem = pl.BlockSpec(memory_space=pltpu.VMEM)
    dma = pltpu.SemaphoreType.DMA
    return pl.pallas_call(
        experts_kernel,
        out_shape=(
            jax.ShapeDtypeStruct(both.shape, bf16),
            jax.ShapeDtypeStruct(own.shape, bf16),
        ),
        in_specs=[anywhere] * 5,
        out_specs=(in_vmem, in_vmem),
        scratch_shapes=[
            pltpu.VMEM((units, features), bf16),
            pltpu.VMEM((units, features), bf16),
            pltpu.VMEM((units, features), bf16),
            pltpu.VMEM((2 * size, features), bf16),
            pltpu.VMEM((3, 4 * size, features), bf16),
            pltpu.VMEM((2 * size, features), bf16),
            pltpu.VMEM((2 * size, features), bf16),
            pltpu.VMEM((3, 4 * size, features), bf16),
            pltpu.VMEM((2 * size, features), bf16),
            pltpu.VMEM((size, features), bf16),
            pltpu.VMEM((3, 2 * size, features), bf16),
            pltpu.VMEM((size, features), bf16),
            pltpu.VMEM((4, 2, 3 * chunk, features), bf16),
            pltpu.VMEM((5, 2, chunk, features), bf16),
            pltpu.VMEM((4 * size, units), bf16),
            dma((5,)),
            dma((4, 2, 3)),
            dma((4, 2, 3)),
            dma((5, 2, 4)),
            dma((5, 2, 4)),
            dma((5, 2)),
            dma((5, 2)),
            dma((5, 2)),
            dma((5, 2)),
            dma((5, 2)),
            dma((5, 2)),
            dma((4, 2, 3)),
            dma((4, 2, 3)),
        ],
        compiler_params=pltpu.CompilerParams(
            collective_id=1, has_side_effects=True, vmem_limit_bytes=60 * 1024 * 1024
        ),
        name="experts",
    )(both, own, gate_weight, up_weight, down_weight)


def body(
    sections,
    columns,
    hidden_in,
    queries,
    new_entries,
    request_cache_rows,
    lengths,
    expert_ids,
    route_weights,
    gate_weight,
    up_weight,
    down_weight,
):
    requests = hidden_in.shape[1]
    attended = attend(queries, new_entries, request_cache_rows, lengths)

    choices = expert_ids.reshape(STEPS, 2 * requests)
    same = choices[:, :, None] == choices[:, None, :]
    earlier = jnp.tril(jnp.ones((2 * requests, 2 * requests), jnp.bool_), -1)
    rank = jnp.sum((same & earlier[None]).astype(jnp.int32), axis=2)
    slot = jnp.arange(STEPS, dtype=jnp.int32)[:, None] * (E * CAP) + choices * CAP + rank
    slot = slot.reshape(STEPS * requests, 2)
    targets = jnp.arange(STEPS * E * CAP, dtype=jnp.int32)
    chosen = slot[:, :, None] == targets[None, None, :]
    selector = jnp.any(chosen, axis=1).astype(jnp.bfloat16).T
    combine = jnp.sum(
        chosen.astype(jnp.float32) * route_weights.reshape(STEPS * requests, 2)[:, :, None], axis=1
    )
    combine = jnp.concatenate([combine[:, : E * CAP]] * sections + [combine[:, E * CAP :]], axis=1)

    both, own = dispatch(attended, hidden_in, selector, sections, columns)
    both, own = run_experts(both, own, gate_weight, up_weight, down_weight)
    return attended, collect(both, own, combine, sections, columns)


def solution(mesh):
    sections, columns = mesh.shape["sec"], mesh.shape["dev"] // LANE
    placed = (
        P(None, ("sec", "dev"), None),
        P(None, ("sec", "dev"), None),
        P(None, ("sec", "dev"), None),
        P(("sec", "dev"), None, None),
        P(("sec", "dev")),
        P(None, ("sec", "dev"), None),
        P(None, ("sec", "dev"), None),
        P("sec", "dev", None),
        P("sec", "dev", None),
        P("sec", "dev", None),
    )
    return jax.shard_map(
        functools.partial(body, sections, columns),
        mesh=mesh,
        in_specs=placed,
        out_specs=(P(None, ("sec", "dev"), None), P(None, ("sec", "dev"), None)),
        check_vma=False,
    )
```

time: 196 us -> 160 us (0.82)
  Pallas kernels: 180 us -> 150 us
  local copies, waits for them, and re-layouts: 12.8 us -> 6.26 us
    pallas_call x3, Pallas kernels: 165 us -> 144 us  [the longest x1 116 us: run_experts(): pl.pallas_call(experts_kernel, out_shape=(jax.ShapeDtypeStruct(both.shape...]
    pallas_call x1, Pallas kernels: 14.8 us -> 5.74 us  [attend(): pl.pallas_call(attend_kernel, out_shape=jax.ShapeDtypeStruct(q.shape, jnp...]
    reshape x5 -> x0, local copies, waits for them, and re-layouts: 6.37 us -> none  [the longest x1 2.43 us: body(): reduced.reshape(sections * columns, SLOTS, features)]
where the time goes in v2:
time: 160 us; the launch traced here: 158 us
  Pallas kernels  150 us (94%)
  local copies, waits for them, and re-layouts  6.26 us (4%)
    pallas_call x1, Pallas kernels, run_experts(): pl.pallas_call(experts_kernel, out_shape=(jax.ShapeDtypeStruct(both.shape...  116 us
    pallas_call x1, Pallas kernels, dispatch(): pl.pallas_call(functools.partial(dispatch_kernel, sections, columns), out...  16.6 us
    pallas_call x1, Pallas kernels, collect(): pl.pallas_call(functools.partial(collect_kernel, sections, columns), out_...  12 us
    pallas_call x1, Pallas kernels, attend(): pl.pallas_call(attend_kernel, out_shape=jax.ShapeDtypeStruct(q.shape, jnp...  5.74 us

profile of v2, /device:TPU:1, one launch (start us, length us, event | category | flops | bytes accessed | tf_op | source)
XLA Modules:
  0.0 158.1 jit_solution(16313014769978521614)
XLA Ops:
  0.6 0.0 copy-start
  0.6 1.0 reshape.63
  1.7 0.7 copy_bitcast_fusion.1.q_ref
  2.3 5.7 %attend.1 = bf16[4,8,16,128]{3,2,1,0:T(8,128)(2,1)} custom-call(s32[4]{0:T(128)} %lengths_ref.1, bf16[4,8,16,128]{3,2,1,0:T(8,128)(2,1)} %copy_bitcast_fusion.1.q_ref, bf16[2,4,2048]{2,1,0:T(4,128)(2,1)} %fresh_ref.1, bf16[4,192,2048]{2,1,0:T(8,128)(2,1)} %cache_ref.1), custom_call_target="tpu_custom_call" | custom-call | tf_op jit(solution)/shard_map/attend/pallas_call | solution.py:85
  8.1 0.9 copy_bitcast_fusion
  9.0 0.7 reshape.66.attended_ref
  9.7 0.0 copy-done
  9.7 0.1 copy.38
  9.8 0.1 eq.28
  9.9 0.1 iota_compare_fusion.1
  10.0 0.2 convert_reduce_fusion
  10.2 0.1 reduce_sum.21
  10.3 0.1 copy.39
  10.4 0.1 mul.30
  10.5 0.1 add.34
  10.5 0.1 add.35
  10.6 0.1 fusion
  10.7 0.7 copy.40
  11.4 16.6 %dispatch.1 = (bf16[32,6144]{1,0:T(8,128)(2,1)}, bf16[16,6144]{1,0:T(8,128)(2,1)}) custom-call(bf16[2,4,6144]{2,1,0:T(4,128)(2,1)} %reshape.66.attended_ref, bf16[2,4,6144]{2,1,0:T(4,128)(2,1)} %hidden_ref.1, bf16[32,8]{1,0:T(8,128)(2,1)} %bitcast.16), custom_call_target="tpu_custom_call" | custom-call | tf_op jit(solution)/shard_map/dispatch/pallas_call | solution.py:205
  28.0 0.0 copy-start.1
  28.0 115.6 %experts.1 = (bf16[32,6144]{1,0:T(8,128)(2,1)}, bf16[16,6144]{1,0:T(8,128)(2,1)}) custom-call(bf16[32,6144]{1,0:T(8,128)(2,1)} %get-tuple-element.6.both_ref, bf16[16,6144]{1,0:T(8,128)(2,1)} %get-tuple-element.7.own_ref, bf16[1,256,6144]{2,1,0:T(8,128)(2,1)} %gate_ref.1, bf16[1,256,6144]{2,1,0:T(8,128)(2,1)} %up_ref.1, bf16[1,256,6144]{2,1,0:T(8,128)(2,1)} %down_ref.1), custom_call_target="tpu_custom_call" | custom-call | tf_op jit(solution)/shard_map/experts/pallas_call | solution.py:596
  143.6 0.0 copy-done.1
  143.7 0.1 mul.31
  143.7 0.1 select_reduce_fusion
  143.8 0.7 pad_maximum_fusion.combine_ref
  144.5 12.0 %collect.1 = bf16[2,4,6144]{2,1,0:T(4,128)(2,1)} custom-call(bf16[32,6144]{1,0:T(8,128)(2,1)} %get-tuple-element.8.both_ref, bf16[16,6144]{1,0:T(8,128)(2,1)} %get-tuple-element.9.own_ref, f32[8,48]{1,0:T(8,128)} %pad_maximum_fusion.combine_ref), custom_call_target="tpu_custom_call" | custom-call | tf_op jit(solution)/shard_map/collect/pallas_call | solution.py:253
  156.5 1.6 copy.46
  (7 shorter events, 0.0 us)
Async XLA Ops:
  0.6 9.1 %copy-start = (s32[2,4,2]{1,2,0:T(2,128)S(1)}, s32[2,4,2]{1,2,0:T(2,128)}, u32[]{:S(2)}) copy-start(s32[2,4,2]{1,2,0:T(2,128)} %param.15) | copy-start | bytes 196
  28.0 115.6 %copy-start.1 = (f32[2,4,2]{1,2,0:T(2,128)S(1)}, f32[2,4,2]{1,2,0:T(2,128)}, u32[]{:S(2)}) copy-start(f32[2,4,2]{1,2,0:T(2,128)} %param.16) | copy-start | bytes 196

commit v3 on v2

--- a/solution.py
+++ b/solution.py
@@ -102,177 +102,19 @@
     return out.transpose(2, 0, 1, 3, 4).reshape(STEPS, requests, QUERY_HEADS * HEAD_SIZE)
 
 
-def exchange_in_plane(
-    sections, columns, both_out, own_out, both_in, own_in, send_sem, recv_sem, local_sem
-):
-    pieces = both_out.shape[0]
-    count = sections * columns
-    device = lax.axis_index("dev")
-    lane = device % LANE
-    section = lax.axis_index("sec")
-    column = device // LANE
-    me = section * columns + column
-    copies = []
-
-    def place(peer):
-        return (peer // columns, (peer % columns) * LANE + lane)
-
-    def greet():
-        barrier = pltpu.get_barrier_semaphore()
-        for offset in range(1, count):
-            pl.semaphore_signal(
-                barrier, inc=1, device_id=place((me + offset) % count), device_id_type=MESH
-            )
-        return lambda: pl.semaphore_wait(barrier, count - 1)
-
-    def send(source, target, where):
-        copies.append(
-            pltpu.make_async_remote_copy(
-                src_ref=source,
-                dst_ref=target,
-                send_sem=send_sem.at[len(copies)],
-                recv_sem=recv_sem.at[len(copies)],
-                device_id=where,
-                device_id_type=MESH,
-            )
-        )
-        copies[-1].start()
-
-    def run():
-        local = [
-            pltpu.make_async_copy(both_out.at[me % pieces], both_in.at[me], local_sem.at[0]),
-            pltpu.make_async_copy(own_out.at[column], own_in.at[column], local_sem.at[1]),
-        ]
-        for copy in local:
-            copy.start()
-        for offset in range(1, columns):
-            peer = (column + offset) % columns
-            send(own_out.at[peer], own_in.at[column], (section, peer * LANE + lane))
-        for offset in range(1, count):
-            peer = (me + offset) % count
-            send(both_out.at[peer % pieces], both_in.at[me], place(peer))
-        for copy in local + copies:
-            copy.wait()
-
-    return greet, run
-
-
-def exchange_scratch(sections, columns, sent, features):
-    count = sections * columns
-    copies = count + columns - 2
-    return [
-        pltpu.VMEM((sent, CAP, features), jnp.bfloat16),
-        pltpu.VMEM((columns, CAP, features), jnp.bfloat16),
-        pltpu.VMEM((count, CAP, features), jnp.bfloat16),
-        pltpu.VMEM((columns, CAP, features), jnp.bfloat16),
-        pltpu.SemaphoreType.DMA((copies,)),
-        pltpu.SemaphoreType.DMA((copies,)),
-        pltpu.SemaphoreType.DMA((2,)),
-    ]
-
-
-def dispatch_kernel(
-    sections, columns, attended_ref, hidden_ref, selector_ref, both_ref, own_ref, *scratch
-):
-    both_out, own_out, both_in, own_in = scratch[:4]
-    greet, run = exchange_in_plane(sections, columns, *scratch)
-    entered = greet()
-    residual_sum = jnp.concatenate(
-        [
-            hidden_ref[t].astype(jnp.float32) + attended_ref[t].astype(jnp.float32)
-            for t in range(STEPS)
-        ],
-        axis=0,
-    )
-    mean_square = jnp.mean(residual_sum * residual_sum, axis=-1, keepdims=True)
-    normed = (residual_sum * lax.rsqrt(mean_square + 1e-05)).astype(jnp.bfloat16)
-    slots = jnp.dot(selector_ref[...], normed, preferred_element_type=jnp.float32)
-    slots = slots.astype(jnp.bfloat16)
-    for e in range(columns):
-        both_out[e] = slots[CAP * e : CAP * (e + 1)]
-        own_out[e] = slots[CAP * (columns + e) : CAP * (columns + e + 1)]
-    entered()
-    run()
-    for j in range(both_in.shape[0]):
-        both_ref[pl.ds(CAP * j, CAP)] = both_in[j]
-    for j in range(columns):
-        own_ref[pl.ds(CAP * j, CAP)] = own_in[j]
-
-
-def dispatch(attended, hidden_in, selector, sections, columns):
-    features = attended.shape[-1]
-    in_vmem = pl.BlockSpec(memory_space=pltpu.VMEM)
-    return pl.pallas_call(
-        functools.partial(dispatch_kernel, sections, columns),
-        out_shape=(
-            jax.ShapeDtypeStruct((sections * columns * CAP, features), jnp.bfloat16),
-            jax.ShapeDtypeStruct((columns * CAP, features), jnp.bfloat16),
-        ),
-        in_specs=[in_vmem] * 3,
-        out_specs=(in_vmem, in_vmem),
-        scratch_shapes=exchange_scratch(sections, columns, columns, features),
-        compiler_params=pltpu.CompilerParams(collective_id=0, has_side_effects=True),
-        name="dispatch",
-    )(attended, hidden_in, selector)
-
-
-def collect_kernel(sections, columns, both_ref, own_ref, combine_ref, out_ref, rows, *scratch):
-    both_out, own_out, both_in, own_in = scratch[:4]
-    greet, run = exchange_in_plane(sections, columns, *scratch)
-    entered = greet()
-    for j in range(both_out.shape[0]):
-        both_out[j] = both_ref[pl.ds(CAP * j, CAP)]
-    for j in range(columns):
-        own_out[j] = own_ref[pl.ds(CAP * j, CAP)]
-    entered()
-    run()
-    count = both_in.shape[0]
-    for j in range(count):
-        rows[pl.ds(CAP * j, CAP)] = both_in[j]
-    for j in range(columns):
-        rows[pl.ds(CAP * (count + j), CAP)] = own_in[j]
-    weights = combine_ref[...]
-    parts = []
-    for _ in range(3):
-        part = weights.astype(jnp.bfloat16)
-        weights = weights - part.astype(jnp.float32)
-        parts.append(part)
-    mixture = jnp.dot(parts[2], rows[...], preferred_element_type=jnp.float32)
-    for part in (parts[1], parts[0]):
-        mixture = mixture + jnp.dot(part, rows[...], preferred_element_type=jnp.float32)
-    requests = out_ref.shape[1]
-    for t in range(STEPS):
-        out_ref[t] = mixture[t * requests : (t + 1) * requests].astype(jnp.bfloat16)
-
-
-def collect(both, own, combine, sections, columns):
-    features = both.shape[-1]
-    requests = combine.shape[0] // STEPS
-    in_vmem = pl.BlockSpec(memory_space=pltpu.VMEM)
-    count = sections * columns
-    return pl.pallas_call(
-        functools.partial(collect_kernel, sections, columns),
-        out_shape=jax.ShapeDtypeStruct((STEPS, requests, features), jnp.bfloat16),
-        in_specs=[in_vmem] * 3,
-        out_specs=in_vmem,
-        scratch_shapes=[pltpu.VMEM(((count + columns) * CAP, features), jnp.bfloat16)]
-        + exchange_scratch(sections, columns, count, features),
-        compiler_params=pltpu.CompilerParams(collective_id=2, has_side_effects=True),
-        name="collect",
-    )(both, own, combine)
-
-
 FIRST, AGAIN, OWN, CROSSED = 0, 1, 2, 3
 
 
 def experts_kernel(
-    both_ref,
-    own_ref,
+    columns,
+    attended_ref,
+    hidden_ref,
+    selector_ref,
+    combine_ref,
     gate_ref,
     up_ref,
     down_ref,
-    both_out,
-    own_out,
+    out_ref,
     gate,
     up,
     down,
@@ -288,7 +130,15 @@
     ring,
     crossed,
     hidden,
+    slot_out,
+    slot_in,
+    sum_out,
+    sum_in,
     load_sem,
+    slot_send,
+    slot_recv,
+    sum_send,
+    sum_recv,
     gather_send,
     gather_recv,
     share_send,
@@ -302,14 +152,15 @@
     reduce_send,
     reduce_recv,
 ):
-    chunk = own_ref.shape[0]
+    chunk = columns * CAP
     size = 4 * chunk
-    features = own_ref.shape[1]
+    features = hidden_ref.shape[-1]
+    narrow = min(512, features)
     wide = min(1024, features)
-    narrow = min(512, features)
     section = lax.axis_index("sec")
     device = lax.axis_index("dev")
-    column, z, core = device // LANE, (device % LANE) // 2, device % 2
+    lane = device % LANE
+    column, z, core = device // LANE, lane // 2, device % 2
 
     def at_z(where):
         return (section, column * LANE + ((where + RING) % RING) * 2 + core)
@@ -331,25 +182,47 @@
         )
 
     loads = [
-        pltpu.make_async_copy(own_ref, rows_0.at[pl.ds(OWN * chunk, chunk)], load_sem.at[0]),
-        pltpu.make_async_copy(both_ref, rows_0.at[pl.ds(0, 2 * chunk)], load_sem.at[1]),
-        pltpu.make_async_copy(gate_ref.at[0], gate, load_sem.at[2]),
-        pltpu.make_async_copy(up_ref.at[0], up, load_sem.at[3]),
-        pltpu.make_async_copy(down_ref.at[0], down, load_sem.at[4]),
+        pltpu.make_async_copy(gate_ref.at[0], gate, load_sem.at[0]),
+        pltpu.make_async_copy(up_ref.at[0], up, load_sem.at[1]),
+        pltpu.make_async_copy(down_ref.at[0], down, load_sem.at[2]),
     ]
     for load in loads:
         load.start()
+    in_plane = [
+        (where, ((column + offset) % columns) * LANE + lane)
+        for where in (section, 1 - section)
+        for offset in range(columns)
+    ][1:]
     barrier = pltpu.get_barrier_semaphore()
-    for where in onward + (partner, opposite):
+    greeted = onward + (partner,) + tuple(in_plane)
+    for where in greeted:
         pl.semaphore_signal(barrier, inc=1, device_id=where, device_id_type=MESH)
-    pl.semaphore_wait(barrier, 4)
-    loads[0].wait()
-    loads[1].wait()
     sends = []
 
     def start(copy):
         copy.start()
         sends.append(copy)
+
+    def exchange(c, source, target, send_sem, recv_sem, local_sem):
+        there = 1 - section if c == AGAIN else section
+        copies = []
+        for offset in range(columns):
+            peer = (column + offset) % columns
+            if c != AGAIN and offset == 0:
+                copy = pltpu.make_async_copy(source.at[peer], target.at[c, column], local_sem)
+                copy.start()
+                copies.append((copy, copy.wait))
+                continue
+            copy = remote(
+                source.at[peer],
+                target.at[c, column],
+                send_sem.at[c, offset],
+                recv_sem.at[c, offset],
+                (there, peer * LANE + lane),
+            )
+            start(copy)
+            copies.append((copy, copy.wait_recv))
+        return [wait for copy, wait in copies]
 
     def block_at(buffers, k, direction, c, of_partner=0):
         at = of_partner * size + c * chunk
@@ -516,7 +389,34 @@
         for direction in directions(k):
             start(pair(k, direction))
 
+    residual_sum = jnp.concatenate(
+        [
+            hidden_ref[t].astype(jnp.float32) + attended_ref[t].astype(jnp.float32)
+            for t in range(STEPS)
+        ],
+        axis=0,
+    )
+    mean_square = jnp.mean(residual_sum * residual_sum, axis=-1, keepdims=True)
+    normed = (residual_sum * lax.rsqrt(mean_square + 1e-05)).astype(jnp.bfloat16)
+    slots = jnp.dot(selector_ref[...], normed, preferred_element_type=jnp.float32)
+    slots = slots.astype(jnp.bfloat16)
+    for t in range(STEPS):
+        for e in range(columns):
+            at = CAP * (t * columns + e)
+            slot_out[t, e] = slots[at : at + CAP]
+    pl.semaphore_wait(barrier, len(greeted))
+    arrivals = {
+        c: exchange(
+            c, slot_out.at[1 if c == OWN else 0], slot_in, slot_send, slot_recv, load_sem.at[3 + c]
+        )
+        for c in (OWN, FIRST, AGAIN)
+    }
+
     for c in (OWN, FIRST, AGAIN):
+        for wait in arrivals[c]:
+            wait()
+        for j in range(columns):
+            rows_0[pl.ds(c * chunk + CAP * j, CAP)] = slot_in[c, j]
         for direction in range(2):
             start(gather(1, direction, c))
         if c == OWN:
@@ -524,7 +424,7 @@
         start(share(0, 0, c))
 
     take_in(1, ringed(1)[:2])
-    for load in loads[2:]:
+    for load in loads:
         load.wait()
     work_on(0)
     take_in(1, ringed(1)[2:])
@@ -556,37 +456,52 @@
             send_sums(k, 1, (FIRST, AGAIN, OWN)[i])
         if k == 2:
             send_crossed_sums(0)
-    for direction in range(2):
-        for c in (FIRST, AGAIN, OWN):
+    arrivals = []
+    for c in (FIRST, AGAIN, OWN):
+        at = pl.ds(c * chunk, chunk)
+        sources = [part_0.at[at], other_0.at[at]]
+        if c == OWN:
+            cross_back(0, 0).wait_recv()
+            sources.append(crossed.at[0, 0])
+        for direction in range(2):
             reduce(1, direction, c).wait_recv()
-    cross_back(0, 0).wait_recv()
-    own_rows = pl.ds(OWN * chunk, chunk)
-    add(
-        own_out,
-        [
-            part_0.at[own_rows],
-            other_0.at[own_rows],
-            crossed.at[0, 0],
-            ring.at[0, 0, own_rows],
-            ring.at[0, 1, own_rows],
-        ],
-    )
-    both_rows = pl.ds(0, 2 * chunk)
-    add(
-        both_out,
-        [
-            part_0.at[both_rows],
-            other_0.at[both_rows],
-            ring.at[0, 0, both_rows],
-            ring.at[0, 1, both_rows],
-        ],
-    )
+            sources.append(ring_at(0, direction, c))
+        add(part_0.at[at], sources)
+        for j in range(columns):
+            sum_out[c, j] = part_0[pl.ds(c * chunk + CAP * j, CAP)]
+        arrivals += exchange(c, sum_out.at[c], sum_in, sum_send, sum_recv, load_sem.at[6 + c])
+    for wait in arrivals:
+        wait()
     for copy in sends:
         copy.wait_send()
-
-
-def run_experts(both, own, gate_weight, up_weight, down_weight):
-    chunk, features = own.shape
+    for c in (FIRST, AGAIN, OWN):
+        for j in range(columns):
+            part_4[pl.ds(c * chunk + CAP * j, CAP)] = sum_in[c, j]
+
+    weights = combine_ref[...]
+    parts = []
+    for _ in range(3):
+        part = weights.astype(jnp.bfloat16)
+        weights = weights - part.astype(jnp.float32)
+        parts.append(part)
+
+    def mix_step(i, carry):
+        at = pl.ds(pl.multiple_of(i * wide, wide), wide)
+        rows = part_4[pl.ds(0, 3 * chunk), at]
+        mixture = jnp.dot(parts[2], rows, preferred_element_type=jnp.float32)
+        for part in (parts[1], parts[0]):
+            mixture = mixture + jnp.dot(part, rows, preferred_element_type=jnp.float32)
+        out_ref[:, at] = mixture.astype(jnp.bfloat16)
+        return carry
+
+    lax.fori_loop(0, features // wide, mix_step, 0)
+
+
+def run_experts(
+    columns, attended, hidden_in, selector, combine, gate_weight, up_weight, down_weight
+):
+    features = hidden_in.shape[-1]
+    chunk = columns * CAP
     size = 4 * chunk
     units = gate_weight.shape[1]
     bf16 = jnp.bfloat16
@@ -594,13 +509,10 @@
     in_vmem = pl.BlockSpec(memory_space=pltpu.VMEM)
     dma = pltpu.SemaphoreType.DMA
     return pl.pallas_call(
-        experts_kernel,
-        out_shape=(
-            jax.ShapeDtypeStruct(both.shape, bf16),
-            jax.ShapeDtypeStruct(own.shape, bf16),
-        ),
-        in_specs=[anywhere] * 5,
-        out_specs=(in_vmem, in_vmem),
+        functools.partial(experts_kernel, columns),
+        out_shape=jax.ShapeDtypeStruct((combine.shape[0], features), bf16),
+        in_specs=[in_vmem] * 4 + [anywhere] * 3,
+        out_specs=in_vmem,
         scratch_shapes=[
             pltpu.VMEM((units, features), bf16),
             pltpu.VMEM((units, features), bf16),
@@ -617,7 +529,15 @@
             pltpu.VMEM((4, 2, 3 * chunk, features), bf16),
             pltpu.VMEM((5, 2, chunk, features), bf16),
             pltpu.VMEM((4 * size, units), bf16),
-            dma((5,)),
+            pltpu.VMEM((STEPS, columns, CAP, features), bf16),
+            pltpu.VMEM((3, columns, CAP, features), bf16),
+            pltpu.VMEM((3, columns, CAP, features), bf16),
+            pltpu.VMEM((3, columns, CAP, features), bf16),
+            dma((9,)),
+            dma((3, columns)),
+            dma((3, columns)),
+            dma((3, columns)),
+            dma((3, columns)),
             dma((4, 2, 3)),
             dma((4, 2, 3)),
             dma((5, 2, 4)),
@@ -632,10 +552,10 @@
             dma((4, 2, 3)),
         ],
         compiler_params=pltpu.CompilerParams(
-            collective_id=1, has_side_effects=True, vmem_limit_bytes=60 * 1024 * 1024
+            collective_id=0, has_side_effects=True, vmem_limit_bytes=60 * 1024 * 1024
         ),
         name="experts",
-    )(both, own, gate_weight, up_weight, down_weight)
+    )(attended, hidden_in, selector, combine, gate_weight, up_weight, down_weight)
 
 
 def body(
@@ -669,9 +589,10 @@
     )
     combine = jnp.concatenate([combine[:, : E * CAP]] * sections + [combine[:, E * CAP :]], axis=1)
 
-    both, own = dispatch(attended, hidden_in, selector, sections, columns)
-    both, own = run_experts(both, own, gate_weight, up_weight, down_weight)
-    return attended, collect(both, own, combine, sections, columns)
+    mixture = run_experts(
+        columns, attended, hidden_in, selector, combine, gate_weight, up_weight, down_weight
+    )
+    return attended, mixture.reshape(hidden_in.shape)
 
 
 def solution(mesh):

time: 160 us -> 149 us (0.931)
  Pallas kernels: 150 us -> 139 us
    pallas_call x3 -> x1, Pallas kernels: 144 us -> 133 us  [run_experts(): pl.pallas_call(functools.partial(experts_kernel, columns), out_shape=jax....]
where the time goes in v3:
time: 149 us
  Pallas kernels  139 us (93%)
  local copies, waits for them, and re-layouts  7.59 us (5%)
  other arithmetic  1.82 us (1%)
    pallas_call x1, Pallas kernels, run_experts(): pl.pallas_call(functools.partial(experts_kernel, columns), out_shape=jax....  133 us
    pallas_call x1, Pallas kernels, attend(): pl.pallas_call(attend_kernel, out_shape=jax.ShapeDtypeStruct(q.shape, jnp...  5.74 us

profile of v3, /device:TPU:1, one launch (start us, length us, event | category | flops | bytes accessed | tf_op | source)
XLA Modules:
  0.0 148.7 jit_solution(1431562272446299135)
XLA Ops:
  0.6 0.1 add.34
  0.7 0.1 add.35
  0.8 0.1 iota_compare_fusion.1
  0.9 0.7 copy.41
  1.6 0.1 mul.31
  1.6 0.7 broadcast_multiply_fusion
  2.3 0.1 mul.30
  2.4 0.8 copy.38
  3.2 0.1 eq.28
  3.3 0.2 convert_reduce_fusion
  3.5 0.1 reduce_sum.21
  3.6 0.1 copy.39
  3.7 0.1 fusion
  3.8 0.1 select_reduce_fusion
  3.8 0.7 pad_maximum_fusion.combine_ref
  4.5 0.7 copy.40
  5.2 1.0 reshape.66
  6.2 0.7 copy_bitcast_fusion.1.q_ref
  6.9 5.7 %attend.1 = bf16[4,8,16,128]{3,2,1,0:T(8,128)(2,1)} custom-call(s32[4]{0:T(128)} %lengths_ref.1, bf16[4,8,16,128]{3,2,1,0:T(8,128)(2,1)} %copy_bitcast_fusion.1.q_ref, bf16[2,4,2048]{2,1,0:T(4,128)(2,1)} %fresh_ref.1, bf16[4,192,2048]{2,1,0:T(8,128)(2,1)} %cache_ref.1), custom_call_target="tpu_custom_call" | custom-call | tf_op jit(solution)/shard_map/attend/pallas_call | solution.py:85
  12.6 0.9 copy_bitcast_fusion
  13.5 0.7 reshape.69.attended_ref
  14.2 132.8 %experts.1 = bf16[8,6144]{1,0:T(8,128)(2,1)} custom-call(bf16[2,4,6144]{2,1,0:T(4,128)(2,1)} %reshape.69.attended_ref, bf16[2,4,6144]{2,1,0:T(4,128)(2,1)} %hidden_ref.1, bf16[32,8]{1,0:T(8,128)(2,1)} %bitcast.16, f32[8,48]{1,0:T(8,128)} %pad_maximum_fusion.combine_ref, bf16[1,256,6144]{2,1,0:T(8,128)(2,1)} %gate_ref.1, bf16[1,256,6144]{2,1,0:T(8,128)(2,1)} %up_ref.1, ...), custom_call_target="tpu_custom_call" | custom-call | tf_op jit(solution)/shard_map/experts/pallas_call | solution.py:511
  147.1 1.6 %reshape.70 = bf16[2,4,6144]{2,1,0:T(4,128)(2,1)} reshape(bf16[8,6144]{1,0:T(8,128)(2,1)} %experts.1) | data formatting | bytes 196608 | tf_op jit(solution)/shard_map/reshape | solution.py:595
  (5 shorter events, 0.0 us)

commit v4 on v3

--- a/solution.py
+++ b/solution.py
@@ -23,7 +23,21 @@
 CONTRACT_LAST = (((1,), (1,)), ((), ()))
 
 
-def attend_kernel(lengths_ref, q_ref, fresh_ref, cache_ref, out_ref, cache, sem):
+def attend_kernel(
+    lengths_ref,
+    experts_ref,
+    weights_ref,
+    q_ref,
+    fresh_ref,
+    cache_ref,
+    out_ref,
+    selector_ref,
+    combine_ref,
+    cache,
+    q_rows,
+    out_rows,
+    sem,
+):
     requests = cache.shape[0]
     rows = STEPS * PADDED_GROUP
     key_width = KEY_VALUE_HEADS * HEAD_SIZE
@@ -33,10 +47,51 @@
     ]
     for load in loads:
         load.start()
+
+    def head_lanes(head, i):
+        return pl.ds((head * GROUP + i) * HEAD_SIZE, HEAD_SIZE)
+
+    q_rows[...] = jnp.zeros_like(q_rows)
+    for head in range(KEY_VALUE_HEADS):
+        for t in range(STEPS):
+            for i in range(GROUP):
+                at = pl.ds((t * PADDED_GROUP + i) * requests, requests)
+                q_rows[head, at] = q_ref[t, :, head_lanes(head, i)].astype(jnp.float32)
+
+    slots, tokens = selector_ref.shape
+    slot_at = lax.broadcasted_iota(jnp.int32, (slots, tokens), 0)
+    token_at = lax.broadcasted_iota(jnp.int32, (slots, tokens), 1)
+    row_at = lax.broadcasted_iota(jnp.int32, combine_ref.shape, 0)
+    column_at = lax.broadcasted_iota(jnp.int32, combine_ref.shape, 1)
+    selector = jnp.zeros((slots, tokens), jnp.float32)
+    combine = jnp.zeros(combine_ref.shape, jnp.float32)
+    for t in range(STEPS):
+        named = []
+        for r in range(requests):
+            token = t * requests + r
+            for j in range(2):
+                expert = experts_ref[t, j, r]
+                rank = jnp.int32(0)
+                for earlier in named:
+                    rank = rank + (earlier == expert).astype(jnp.int32)
+                named.append(expert)
+                slot = expert * CAP + rank
+                selector = jnp.where(
+                    (slot_at == slot + t * E * CAP) & (token_at == token), 1.0, selector
+                )
+                if t == 0:
+                    here = (column_at == slot) | (column_at == slot + E * CAP)
+                else:
+                    here = column_at == slot + 2 * E * CAP
+                combine = jnp.where(here & (row_at == token), weights_ref[t, j, r], combine)
+    selector_ref[...] = selector.astype(jnp.bfloat16)
+    combine_ref[...] = combine
+
     every = KEY_VALUE_HEADS * rows
     place = lax.broadcasted_iota(jnp.int32, (every, LONGEST_LENGTH), 1)
     second = (lax.broadcasted_iota(jnp.int32, (every, 1), 0) // PADDED_GROUP) % STEPS == 1
     for r in range(requests):
+        of_request = pl.ds(r, rows, stride=requests)
         fresh_keys, fresh_values = [], []
         for t in range(STEPS):
             entry = fresh_ref[t, pl.ds(r, 1), :].astype(jnp.float32)
@@ -46,13 +101,15 @@
         past, fresh = [], [[] for t in range(STEPS)]
         for head in range(KEY_VALUE_HEADS):
             lanes = slice(head * HEAD_SIZE, (head + 1) * HEAD_SIZE)
-            q = q_ref[r, head]
+            wide = q_rows[head, of_request, :]
             past.append(
                 lax.dot_general(
-                    q, cache[r, :, lanes], CONTRACT_LAST, preferred_element_type=jnp.float32
+                    wide.astype(jnp.bfloat16),
+                    cache[r, :, lanes],
+                    CONTRACT_LAST,
+                    preferred_element_type=jnp.float32,
                 )
             )
-            wide = q.astype(jnp.float32)
             for t in range(STEPS):
                 fresh[t].append(jnp.sum(wide * fresh_keys[t][:, lanes], axis=1, keepdims=True))
         past = jnp.concatenate(past, axis=0) * scale
@@ -72,34 +129,43 @@
             mixed = jnp.dot(past[here], cache[r, :, values], preferred_element_type=jnp.float32)
             for t in range(STEPS):
                 mixed = mixed + fresh[t][here] * fresh_values[t][:, lanes]
-            out_ref[r, head] = mixed.astype(jnp.bfloat16)
-
-
-def attend(queries, new_entries, request_cache_rows, lengths):
-    requests = queries.shape[1]
-    rows = STEPS * PADDED_GROUP
-    q = queries.reshape(STEPS, requests, KEY_VALUE_HEADS, GROUP, HEAD_SIZE)
-    q = jnp.pad(q, ((0, 0), (0, 0), (0, 0), (0, PADDED_GROUP - GROUP), (0, 0)))
-    q = q.transpose(1, 2, 0, 3, 4).reshape(requests, KEY_VALUE_HEADS, rows, HEAD_SIZE)
+            out_rows[head, of_request, :] = mixed
+    for head in range(KEY_VALUE_HEADS):
+        for t in range(STEPS):
+            for i in range(GROUP):
+                at = pl.ds((t * PADDED_GROUP + i) * requests, requests)
+                out_ref[t, :, head_lanes(head, i)] = out_rows[head, at].astype(jnp.bfloat16)
+
+
+def attend(queries, new_entries, request_cache_rows, lengths, expert_ids, route_weights):
+    steps, requests, features = queries.shape
+    rows = STEPS * PADDED_GROUP * requests
     in_vmem = pl.BlockSpec(memory_space=pltpu.VMEM)
-    out = pl.pallas_call(
+    in_smem = pl.BlockSpec(memory_space=pltpu.SMEM)
+    return pl.pallas_call(
         attend_kernel,
-        out_shape=jax.ShapeDtypeStruct(q.shape, jnp.bfloat16),
-        in_specs=[
-            pl.BlockSpec(memory_space=pltpu.SMEM),
-            in_vmem,
-            in_vmem,
-            pl.BlockSpec(memory_space=pl.ANY),
-        ],
-        out_specs=in_vmem,
+        out_shape=(
+            jax.ShapeDtypeStruct(queries.shape, jnp.bfloat16),
+            jax.ShapeDtypeStruct((STEPS * E * CAP, STEPS * requests), jnp.bfloat16),
+            jax.ShapeDtypeStruct((STEPS * requests, 3 * E * CAP), jnp.float32),
+        ),
+        in_specs=[in_smem] * 3 + [in_vmem] * 2 + [pl.BlockSpec(memory_space=pl.ANY)],
+        out_specs=(in_vmem,) * 3,
         scratch_shapes=[
             pltpu.VMEM(request_cache_rows.shape, jnp.bfloat16),
+            pltpu.VMEM((KEY_VALUE_HEADS, rows, HEAD_SIZE), jnp.float32),
+            pltpu.VMEM((KEY_VALUE_HEADS, rows, HEAD_SIZE), jnp.float32),
             pltpu.SemaphoreType.DMA((requests,)),
         ],
         name="attend",
-    )(lengths, q, new_entries, request_cache_rows)
-    out = out.reshape(requests, KEY_VALUE_HEADS, STEPS, PADDED_GROUP, HEAD_SIZE)[:, :, :, :GROUP]
-    return out.transpose(2, 0, 1, 3, 4).reshape(STEPS, requests, QUERY_HEADS * HEAD_SIZE)
+    )(
+        lengths,
+        expert_ids.transpose(0, 2, 1),
+        route_weights.transpose(0, 2, 1),
+        queries,
+        new_entries,
+        request_cache_rows,
+    )
 
 
 FIRST, AGAIN, OWN, CROSSED = 0, 1, 2, 3
@@ -559,7 +625,6 @@
 
 
 def body(
-    sections,
     columns,
     hidden_in,
     queries,
@@ -572,23 +637,9 @@
     up_weight,
     down_weight,
 ):
-    requests = hidden_in.shape[1]
-    attended = attend(queries, new_entries, request_cache_rows, lengths)
-
-    choices = expert_ids.reshape(STEPS, 2 * requests)
-    same = choices[:, :, None] == choices[:, None, :]
-    earlier = jnp.tril(jnp.ones((2 * requests, 2 * requests), jnp.bool_), -1)
-    rank = jnp.sum((same & earlier[None]).astype(jnp.int32), axis=2)
-    slot = jnp.arange(STEPS, dtype=jnp.int32)[:, None] * (E * CAP) + choices * CAP + rank
-    slot = slot.reshape(STEPS * requests, 2)
-    targets = jnp.arange(STEPS * E * CAP, dtype=jnp.int32)
-    chosen = slot[:, :, None] == targets[None, None, :]
-    selector = jnp.any(chosen, axis=1).astype(jnp.bfloat16).T
-    combine = jnp.sum(
-        chosen.astype(jnp.float32) * route_weights.reshape(STEPS * requests, 2)[:, :, None], axis=1
+    attended, selector, combine = attend(
+        queries, new_entries, request_cache_rows, lengths, expert_ids, route_weights
     )
-    combine = jnp.concatenate([combine[:, : E * CAP]] * sections + [combine[:, E * CAP :]], axis=1)
-
     mixture = run_experts(
         columns, attended, hidden_in, selector, combine, gate_weight, up_weight, down_weight
     )
@@ -596,7 +647,7 @@
 
 
 def solution(mesh):
-    sections, columns = mesh.shape["sec"], mesh.shape["dev"] // LANE
+    columns = mesh.shape["dev"] // LANE
     placed = (
         P(None, ("sec", "dev"), None),
         P(None, ("sec", "dev"), None),
@@ -610,7 +661,7 @@
         P("sec", "dev", None),
     )
     return jax.shard_map(
-        functools.partial(body, sections, columns),
+        functools.partial(body, columns),
         mesh=mesh,
         in_specs=placed,
         out_specs=(P(None, ("sec", "dev"), None), P(None, ("sec", "dev"), None)),

time: 149 us -> 141 us (0.946)
  local copies, waits for them, and re-layouts: 7.59 us -> 1.58 us
  other arithmetic: 1.82 us -> 0 us
    reshape x3 -> x0, local copies, waits for them, and re-layouts: 2.38 us -> none  [the longest x1 1.01 us: attend(): q = queries.reshape(STEPS, requests, KEY_VALUE_HEADS, GROUP, HEAD_SIZE)]
where the time goes in v4:
time: 141 us
  Pallas kernels  139 us (99%)
  local copies, waits for them, and re-layouts  1.58 us (1%)
    pallas_call x1, Pallas kernels, run_experts(): pl.pallas_call(functools.partial(experts_kernel, columns), out_shape=jax....  133 us
    pallas_call x1, Pallas kernels, attend(): pl.pallas_call(attend_kernel, out_shape=(jax.ShapeDtypeStruct(queries.sha...  5.74 us

profile of v4, /device:TPU:1, one launch (start us, length us, event | category | flops | bytes accessed | tf_op | source)
XLA Modules:
  0.0 141.0 jit_solution(8430557598866583349)
XLA Ops:
  0.6 5.7 %attend.1 = (bf16[2,4,6144]{2,1,0:T(4,128)(2,1)}, bf16[32,8]{1,0:T(8,128)(2,1)}, f32[8,48]{1,0:T(8,128)}) custom-call(s32[4]{0:T(128)} %lengths_ref.1, s32[2,2,4]{2,1,0:T(2,128)} %bitcast.2, f32[2,2,4]{2,1,0:T(2,128)} %bitcast.3, bf16[2,4,6144]{2,1,0:T(4,128)(2,1)} %q_ref.1, bf16[2,4,2048]{2,1,0:T(4,128)(2,1)} %fresh_ref.1, bf16[4,192,2048]{2,1,0:T(8,128)(2,1)} %cache_ref.1), custom_call_target="tpu_custom_call" | custom-call | tf_op jit(solution)/shard_map/attend/pallas_call | solution.py:145
  6.4 133.0 %experts.1 = bf16[8,6144]{1,0:T(8,128)(2,1)} custom-call(bf16[2,4,6144]{2,1,0:T(4,128)(2,1)} %get-tuple-element.3.attended_ref, bf16[2,4,6144]{2,1,0:T(4,128)(2,1)} %hidden_ref.1, bf16[32,8]{1,0:T(8,128)(2,1)} %get-tuple-element.6.selector_ref, f32[8,48]{1,0:T(8,128)} %get-tuple-element.7.combine_ref, bf16[1,256,6144]{2,1,0:T(8,128)(2,1)} %gate_ref.1, ...), custom_call_target="tpu_custom_call" | custom-call | tf_op jit(solution)/shard_map/experts/pallas_call | solution.py:577
  139.4 1.6 %reshape.7 = bf16[2,4,6144]{2,1,0:T(4,128)(2,1)} reshape(bf16[8,6144]{1,0:T(8,128)(2,1)} %experts.1) | data formatting | bytes 196608 | tf_op jit(solution)/shard_map/reshape | solution.py:646

commit v5 on v4

--- a/solution.py
+++ b/solution.py
@@ -341,7 +341,7 @@
     def home(k, direction):
         return direction if 0 < k < 4 else 0
 
-    def multiply(rows, part):
+    def multiply_in(rows):
         count = rows.shape[0]
 
         x = rows[...]
@@ -351,6 +351,9 @@
             x, up[...], CONTRACT_LAST, preferred_element_type=jnp.float32
         )
         hidden[pl.ds(0, count)] = value.astype(jnp.bfloat16)
+
+    def multiply_out(part):
+        count = part.shape[0]
 
         def output_step(i, carry):
             at = pl.ds(pl.multiple_of(i * wide, wide), wide)
@@ -446,12 +449,10 @@
         for direction in directions(k):
             for c in range(4):
                 share(k, direction, c).wait_recv()
-        if k == 0:
-            multiply(rows_0, part_0)
-        elif k == 4:
-            multiply(rows_4, part_4)
-        else:
-            multiply(rows_mid.at[k - 1], part_mid.at[k - 1])
+        multiply_in(rows_0 if k == 0 else rows_4 if k == 4 else rows_mid.at[k - 1])
+
+    def finish(k):
+        multiply_out(part_0 if k == 0 else part_4 if k == 4 else part_mid.at[k - 1])
         for direction in directions(k):
             start(pair(k, direction))
 
@@ -492,21 +493,22 @@
     take_in(1, ringed(1)[:2])
     for load in loads:
         load.wait()
-    work_on(0)
-    take_in(1, ringed(1)[2:])
-    take_in(2, ringed(2)[:2])
-    work_on(1)
-    take_in(2, ringed(2)[2:])
-    take_in(3, ringed(3)[:2])
-    work_on(2)
-    take_in(3, ringed(3)[2:])
+    for k in range(1, 4):
+        if k > 1:
+            take_in(k, ringed(k)[:2])
+        work_on(k - 1)
+        take_in(k, ringed(k)[2:4])
+        finish(k - 1)
+        take_in(k, ringed(k)[4:])
     take_in(4, ringed(4)[:1])
     work_on(3)
+    finish(3)
     send_crossed_sums(3)
     take_in(4, ringed(4)[1:])
     for direction, c in ((1, FIRST), (1, AGAIN), (0, OWN)):
         send_sums(3, direction, c, from_ring=False)
     work_on(4)
+    finish(4)
 
     send_crossed_sums(4)
     send_sums(4, 0, FIRST, from_ring=False)

time: 141 us -> 139 us (0.986)
  the two profiles are of different devices: /device:TPU:1 before, /device:TPU:38 now
where the time goes in v5:
time: 139 us
  Pallas kernels  137 us (99%)
  local copies, waits for them, and re-layouts  1.58 us (1%)
    pallas_call x1, Pallas kernels, run_experts(): pl.pallas_call(functools.partial(experts_kernel, columns), out_shape=jax....  131 us
    pallas_call x1, Pallas kernels, attend(): pl.pallas_call(attend_kernel, out_shape=(jax.ShapeDtypeStruct(queries.sha...  5.74 us

profile of v5, /device:TPU:38, one launch (start us, length us, event | category | flops | bytes accessed | tf_op | source)
XLA Modules:
  0.0 139.3 jit_solution(16344409485690379584)
XLA Ops:
  0.6 5.7 %attend.1 = (bf16[2,4,6144]{2,1,0:T(4,128)(2,1)}, bf16[32,8]{1,0:T(8,128)(2,1)}, f32[8,48]{1,0:T(8,128)}) custom-call(s32[4]{0:T(128)} %lengths_ref.1, s32[2,2,4]{2,1,0:T(2,128)} %bitcast.2, f32[2,2,4]{2,1,0:T(2,128)} %bitcast.3, bf16[2,4,6144]{2,1,0:T(4,128)(2,1)} %q_ref.1, bf16[2,4,2048]{2,1,0:T(4,128)(2,1)} %fresh_ref.1, bf16[4,192,2048]{2,1,0:T(8,128)(2,1)} %cache_ref.1), custom_call_target="tpu_custom_call" | custom-call | tf_op jit(solution)/shard_map/attend/pallas_call | solution.py:145
  6.4 131.3 %experts.1 = bf16[8,6144]{1,0:T(8,128)(2,1)} custom-call(bf16[2,4,6144]{2,1,0:T(4,128)(2,1)} %get-tuple-element.3.attended_ref, bf16[2,4,6144]{2,1,0:T(4,128)(2,1)} %hidden_ref.1, bf16[32,8]{1,0:T(8,128)(2,1)} %get-tuple-element.6.selector_ref, f32[8,48]{1,0:T(8,128)} %get-tuple-element.7.combine_ref, bf16[1,256,6144]{2,1,0:T(8,128)(2,1)} %gate_ref.1, ...), custom_call_target="tpu_custom_call" | custom-call | tf_op jit(solution)/shard_map/experts/pallas_call | solution.py:579
  137.7 1.6 %reshape.7 = bf16[2,4,6144]{2,1,0:T(4,128)(2,1)} reshape(bf16[8,6144]{1,0:T(8,128)(2,1)} %experts.1) | data formatting | bytes 196608 | tf_op jit(solution)/shard_map/reshape | solution.py:648
